TPU v7x, 32 devices: a whole 2x2x4 slice. The times are simulated.
32 devices in a mesh: rep: 2 (over x), exp: 2 (over core), tp: 8 (over z, y).
Axes of the slice: x: 2, y: 2, z: 4, core: 2. Of those that a mesh axis runs over, the one named last changes fastest.
Arguments:
- tokens: bfloat16 [128, 4096], P(('rep', 'exp', 'tp')), parts along dimension 0, may hold values from -6 to 6
- expert_ids: int32 [128, 2], P(('rep', 'exp', 'tp')), parts along dimension 0, may hold values from 0 to 3, all different within a row; in each aligned block of 4 rows (0 to 3, 4 to 7, ...) at most 4 rows name the same one
- gate_ints: int32 [128, 2], P(('rep', 'exp', 'tp')), parts along dimension 0, may hold values from 16 to 240, as said below
- gate_weight: bfloat16 [4, 4096, 14336], P('exp', None, 'tp'), may hold values from -0.09375 to 0.09375
- up_weight: bfloat16 [4, 4096, 14336], P('exp', None, 'tp'), may hold values from -0.09375 to 0.09375
- down_weight: bfloat16 [4, 14336, 4096], P('exp', 'tp'), may hold values from -0.046875 to 0.046875
Outputs:
- mixed: bfloat16 [128, 4096], P(('rep', 'exp', 'tp')), parts along dimension 0
There are 2 independent parts, one for each index of `rep`. A program takes and returns all parts, laid end to end along the dimension named above; an argument that names none is the same for every part. Nothing has to cross between parts.
Inputs may be any that keep to these rules, and one draw needn't show every extreme that they name: `expert_ids`: each row names two different experts. Among the 4 rows of one device an expert is named at most 4 times, and exactly that often on some device. `gate_ints`: the two entries of a row sum to 256.
All inputs are finite; a program needn't handle non-finite values.
Results may differ from a plain program's by a relative error of at most 0.0049.
Values may be sent and summed in bfloat16 or wider, within the bound.
A program may use at most 128 MiB of HBM per device.

v0:
```python
import functools

import jax
import jax.numpy as jnp
from jax import lax
from jax.experimental import pallas as pl
from jax.experimental.pallas import tpu as pltpu
from jax.sharding import PartitionSpec as P

MESH = pl.DeviceIdType.MESH
LANES = 128
VMEM_BYTES = 67043328


def kernel(
    nt, fb, cw, gu_slots, dn_slots,
    ids_ref, gates_ref, tok_ref, gw_ref, uw_ref, dw_ref, out_ref,
    xg, stage, x, wst, h, gu_buf, dn_buf,
    part, ex_send, ex_recv, tp_send, tp_recv,
    gu_sem, dn_sem, ga_send, ga_fwd, ga_recv, ex_ssem, ex_rsem, tp_ssem, tp_rsem,
):
    e = lax.axis_index("exp")
    t = lax.axis_index("tp")
    other = 1 - e
    me = e * nt + t
    rows, width = tok_ref.shape
    experts, _, hidden = gw_ref.shape
    tokens = x.shape[0]
    half = tokens // 2
    nf = hidden // fb
    nc = width // cw
    gu_steps = experts * nf

    def gu_copies(i, slot):
        l = i // nf
        columns = pl.ds(pl.multiple_of((i % nf) * fb, fb), fb) if nf > 1 else slice(None)
        return [
            pltpu.make_async_copy(
                ref.at[l, :, columns], gu_buf.at[slot, m], gu_sem.at[slot, m]
            )
            for m, ref in enumerate((gw_ref, uw_ref))
        ]

    def dn_copies(c, slot):
        c0 = pl.multiple_of(c * cw, cw)
        return [
            pltpu.make_async_copy(
                dw_ref.at[l, :, pl.ds(c0, cw)], dn_buf.at[slot, l], dn_sem.at[slot, l]
            )
            for l in range(experts)
        ]

    def first(i, carry):
        for copy in gu_copies(i, i):
            copy.start()
        return carry

    lax.fori_loop(0, gu_slots, first, 0)

    barrier = pltpu.get_barrier_semaphore()

    def greet(d, carry):
        pl.semaphore_signal(
            barrier, inc=1, device_id={"tp": (t + d) % nt}, device_id_type=MESH
        )
        return carry

    lax.fori_loop(1, nt, greet, 0)
    pl.semaphore_signal(barrier, inc=1, device_id={"exp": other}, device_id_type=MESH)

    lane = lax.broadcasted_iota(jnp.int32, (rows, LANES), 1)
    sub = lax.broadcasted_iota(jnp.int32, (rows, LANES), 0)
    weight = jnp.zeros((rows, LANES), jnp.float32)
    for r in range(rows):
        for k in range(ids_ref.shape[0]):
            value = gates_ref[k, r].astype(jnp.float32) * (1.0 / 256.0)
            weight += jnp.where((sub == r) & (lane == ids_ref[k, r]), value, 0.0)
    xg[me, :, :width] = tok_ref[...]
    xg[me, :, width:] = weight.astype(jnp.bfloat16)

    pl.semaphore_wait(barrier, nt)

    def to_other(tt):
        slot = e * nt + tt
        return pltpu.make_async_remote_copy(
            src_ref=xg.at[slot], dst_ref=xg.at[slot],
            send_sem=ga_fwd.at[tt], recv_sem=ga_recv.at[slot],
            device_id={"exp": other}, device_id_type=MESH,
        )

    def to_tp(d):
        return pltpu.make_async_remote_copy(
            src_ref=xg.at[me], dst_ref=xg.at[me],
            send_sem=ga_send.at[d], recv_sem=ga_recv.at[me],
            device_id={"tp": (t + d) % nt}, device_id_type=MESH,
        )

    def from_slot(slot):
        return pltpu.make_async_remote_copy(
            src_ref=xg.at[slot], dst_ref=xg.at[slot],
            send_sem=ga_send.at[0], recv_sem=ga_recv.at[slot],
            device_id={"exp": other}, device_id_type=MESH,
        )

    def push(d, carry):
        to_tp(d).start()
        return carry

    lax.fori_loop(1, nt, push, 0)
    to_other(t).start()

    def relay(d, carry):
        source = (t + nt - d) % nt
        from_slot(e * nt + source).wait_recv()
        to_other(source).start()
        return carry

    lax.fori_loop(1, nt, relay, 0)

    def arrive(tt, carry):
        from_slot(other * nt + tt).wait_recv()
        return carry

    lax.fori_loop(0, nt, arrive, 0)

    group = stage.shape[0] // rows

    def lay(g, carry):
        for i in range(group):
            stage[i * rows:(i + 1) * rows, :] = xg[g * group + i].astype(jnp.float32)
        r0 = pl.multiple_of(g * group * rows, group * rows)
        x[pl.ds(r0, group * rows), :] = stage[:, :width].astype(jnp.bfloat16)
        wst[pl.ds(r0, group * rows), :] = stage[:, width:]
        return carry

    lax.fori_loop(0, tokens // (group * rows), lay, 0)

    def gu_step(i, carry):
        slot = i % gu_slots
        for copy in gu_copies(i, slot):
            copy.wait()
        gate, upper = (
            jnp.dot(x[...], gu_buf[slot, m], preferred_element_type=jnp.float32) for m in range(2)
        )
        columns = pl.ds(pl.multiple_of((i % nf) * fb, fb), fb) if nf > 1 else slice(None)
        h[i // nf, :, columns] = (gate / (1.0 + jnp.exp(-gate)) * upper).astype(jnp.bfloat16)
        later = i + gu_slots

        @pl.when(later < gu_steps)
        def _():
            for copy in gu_copies(later, slot):
                copy.start()

        column = later - gu_steps

        @pl.when((column >= 0) & (column < dn_slots))
        def _():
            for copy in dn_copies(column, column):
                copy.start()

        return carry

    lax.fori_loop(0, gu_steps, gu_step, 0)

    lanes = lax.broadcasted_iota(jnp.int32, (tokens, LANES), 1)
    scales = [
        jnp.sum(jnp.where(lanes == e * experts + l, wst[...], 0.0), axis=1, keepdims=True)
        for l in range(experts)
    ]

    def ex_copy(c):
        return pltpu.make_async_remote_copy(
            src_ref=ex_send.at[c], dst_ref=ex_recv.at[c],
            send_sem=ex_ssem.at[c], recv_sem=ex_rsem.at[c],
            device_id={"exp": other}, device_id_type=MESH,
        )

    def tp_copy(c, d):
        target = (t + d) % nt
        return pltpu.make_async_remote_copy(
            src_ref=tp_send.at[c, target], dst_ref=tp_recv.at[c, t],
            send_sem=tp_ssem.at[c, d], recv_sem=tp_rsem.at[c, t],
            device_id={"tp": target}, device_id_type=MESH,
        )

    def tp_from(c, source):
        return pltpu.make_async_remote_copy(
            src_ref=tp_send.at[c, source], dst_ref=tp_recv.at[c, source],
            send_sem=tp_ssem.at[c, 0], recv_sem=tp_rsem.at[c, source],
            device_id={"tp": source}, device_id_type=MESH,
        )

    def pass_on(c):
        ex_copy(c).wait_recv()
        total = part[c, e] + ex_recv[c].astype(jnp.float32)
        for j in range(nt):
            tp_send[c, j] = total[j * rows:(j + 1) * rows, :].astype(jnp.bfloat16)
        tp_recv[c, t] = tp_send[c, t]

        def send(d, carry):
            tp_copy(c, d).start()
            return carry

        lax.fori_loop(1, nt, send, 0)

    def dn_step(c, carry):
        slot = c % dn_slots
        for copy in dn_copies(c, slot):
            copy.wait()
        for n in range(0, cw, 256):
            size = min(256, cw - n)
            total = jnp.zeros((tokens, size), jnp.float32)
            for l in range(experts):
                total += scales[l] * jnp.dot(
                    h[l], dn_buf[slot, l, :, n:n + size], preferred_element_type=jnp.float32
                )
            part[c, 0, :, n:n + size] = total[:half]
            part[c, 1, :, n:n + size] = total[half:]
        ex_send[c] = part[c, other].astype(jnp.bfloat16)
        ex_copy(c).start()
        later = c + dn_slots

        @pl.when(later < nc)
        def _():
            for copy in dn_copies(later, slot):
                copy.start()

        @pl.when(c > 0)
        def _():
            pass_on(c - 1)

        return carry

    lax.fori_loop(0, nc, dn_step, 0)
    pass_on(nc - 1)

    for c in range(nc):
        def collect(d, carry, c=c):
            tp_from(c, (t + nt - d) % nt).wait_recv()
            return carry

        lax.fori_loop(1, nt, collect, 0)
        total = tp_recv[c, 0].astype(jnp.float32)
        for j in range(1, nt):
            total += tp_recv[c, j].astype(jnp.float32)
        out_ref[:, c * cw:(c + 1) * cw] = total.astype(out_ref.dtype)

    def finish(d, carry):
        to_tp(d).wait_send()
        to_other((t + d) % nt).wait_send()

        def drain(c, inner):
            tp_copy(c, d).wait_send()
            return inner

        lax.fori_loop(0, nc, drain, 0)
        return carry

    lax.fori_loop(1, nt, finish, 0)
    to_other(t).wait_send()

    def drain_ex(c, carry):
        ex_copy(c).wait_send()
        return carry

    lax.fori_loop(0, nc, drain_ex, 0)


def body(tokens, expert_ids, gate_ints, gate_weight, up_weight, down_weight):
    rows, width = tokens.shape
    experts, _, hidden = gate_weight.shape
    nt = lax.axis_size("tp")
    slots = nt * lax.axis_size("exp")
    total = slots * rows
    fb = 256 if hidden % 256 == 0 else hidden
    cw = min(512, width)
    nf, nc = hidden // fb, width // cw
    gu_slots = min(8, experts * nf)
    dn_slots = min(7, nc)
    bf16, f32 = jnp.bfloat16, jnp.float32
    vmem = pl.BlockSpec(memory_space=pltpu.VMEM)
    smem = pl.BlockSpec(memory_space=pltpu.SMEM)
    hbm = pl.BlockSpec(memory_space=pl.ANY)
    dma = pltpu.SemaphoreType.DMA
    return pl.pallas_call(
        functools.partial(kernel, nt, fb, cw, gu_slots, dn_slots),
        out_shape=jax.ShapeDtypeStruct((rows, width), bf16),
        in_specs=[smem, smem, vmem, hbm, hbm, hbm],
        out_specs=vmem,
        scratch_shapes=[
            pltpu.VMEM((slots, rows, width + LANES), bf16),
            pltpu.VMEM((16, width + LANES), f32),
            pltpu.VMEM((total, width), bf16),
            pltpu.VMEM((total, LANES), f32),
            pltpu.VMEM((experts, total, hidden), bf16),
            pltpu.VMEM((gu_slots, 2, width, fb), bf16),
            pltpu.VMEM((dn_slots, experts, hidden, cw), bf16),
            pltpu.VMEM((nc, 2, total // 2, cw), f32),
            pltpu.VMEM((nc, total // 2, cw), bf16),
            pltpu.VMEM((nc, total // 2, cw), bf16),
            pltpu.VMEM((nc, nt, rows, cw), bf16),
            pltpu.VMEM((nc, nt, rows, cw), bf16),
            dma((gu_slots, 2)),
            dma((dn_slots, experts)),
            dma((nt,)),
            dma((nt,)),
            dma((slots,)),
            dma((nc,)),
            dma((nc,)),
            dma((nc, nt)),
            dma((nc, nt)),
        ],
        compiler_params=pltpu.CompilerParams(
            collective_id=0, has_side_effects=True, vmem_limit_bytes=VMEM_BYTES
        ),
    )(expert_ids.T, gate_ints.T, tokens, gate_weight, up_weight, down_weight)


def solution(mesh):
    return jax.shard_map(
        body,
        mesh=mesh,
        in_specs=(
            P(("rep", "exp", "tp"), None),
            P(("rep", "exp", "tp"), None),
            P(("rep", "exp", "tp"), None),
            P("exp", None, "tp"),
            P("exp", None, "tp"),
            P("exp", "tp", None),
        ),
        out_specs=P(("rep", "exp", "tp"), None),
        check_vma=False,
    )
```

profile of v0, /device:TPU:0, one launch (start us, length us, event | category | flops | bytes accessed | tf_op | source)
XLA Modules:
  0.0 44.9 jit_solution(17332515548030766312)
XLA Ops:
  0.0 43.5 %shard_map.64 = bf16[4,4096]{1,0:T(4,128)(2,1)} custom-call(s32[2,4]{1,0:T(2,128)} %bitcast.2, s32[2,4]{1,0:T(2,128)} %bitcast.3, bf16[4,4096]{1,0:T(4,128)(2,1)} %tok_ref.1, bf16[2,4096,1792]{2,1,0:T(8,128)(2,1)} %gw_ref.1, bf16[2,4096,1792]{2,1,0:T(8,128)(2,1)} %uw_ref.1, bf16[2,1792,4096]{2,1,0:T(8,128)(2,1)} %dw_ref.1), custom_call_target="tpu_custom_call" | custom-call | tf_op jit(solution)/shard_map/pallas_call | solution.py:285
  43.5 1.4 %copy.8 = bf16[4,4096]{1,0:T(4,128)(2,1)} copy(bf16[4,4096]{1,0:T(4,128)(2,1)} %shard_map.64) | data formatting | bytes 65536
where the time goes:
time: 45.1 us; the launch traced here: 44.9 us
  Pallas kernels  43.5 us (96%)
  local copies, waits for them, and re-layouts  1.39 us (3%)
    pallas_call x1, Pallas kernels, body(): pl.pallas_call(functools.partial(kernel, nt, fb, cw, gu_slots, dn_slots),...  43.5 us
    unnamed x1, local copies, waits for them, and re-layouts  1.39 us

commit v1 on v0

v1 whole, which is shorter than its diff:
```python
import functools

import jax
import jax.numpy as jnp
from jax import lax
from jax.experimental import pallas as pl
from jax.experimental.pallas import tpu as pltpu
from jax.sharding import PartitionSpec as P

MESH = pl.DeviceIdType.MESH
LANES = 128
VMEM_BYTES = 67043328


def kernel(
    dims, kc, cw, window,
    ids_ref, gates_ref, tok_ref, gw_ref, uw_ref, dw_ref, out_ref,
    xg, stage, x, wst, acc, h, wbuf, dbuf, keep, mine,
    ex_send, ex_recv, rp_send, rp_recv, tp_send, tp_recv,
    gu_sem, dn_sem, zs, rs, ys, es, g_recv,
    ex_ssem, ex_rsem, rp_ssem, rp_rsem, tp_ssem, tp_rsem,
):
    nr, nz, ny, own = dims
    nt = nz * ny
    r = lax.axis_index("rep")
    e = lax.axis_index("exp")
    t = lax.axis_index("tp")
    z, y = t // ny, t % ny
    other = 1 - e
    rows, width = tok_ref.shape
    hidden = gw_ref.shape[2]
    experts = gw_ref.shape[0]
    nk, tokens, _ = x.shape
    half = tokens // 2
    quarter = nt * rows
    nc = width // cw
    group = stage.shape[0] // rows

    def slot_of(ee, rr, tt):
        return (ee * nr + rr) * nt + tt

    me = slot_of(e, r, t)

    def gu_copies(l, k):
        return [
            pltpu.make_async_copy(
                ref.at[r * own + l, pl.ds(k * kc, kc), :],
                wbuf.at[l, m, pl.ds(k * kc, kc), :],
                gu_sem.at[l, m, k],
            )
            for m, ref in enumerate((gw_ref, uw_ref))
        ]

    def dn_copies(c):
        return [
            pltpu.make_async_copy(
                dw_ref.at[r * own + l, :, pl.ds(c * cw, cw)], dbuf.at[l, c], dn_sem.at[l, c]
            )
            for l in range(own)
        ]

    items = [functools.partial(gu_copies, l, k) for l in range(own) for k in range(nk)]
    items += [functools.partial(dn_copies, c) for c in range(nc)]
    waited = [0]

    def start(i):
        if i < len(items):
            for copy in items[i]():
                copy.start()

    def pump(upto):
        while waited[0] < upto:
            for copy in items[waited[0]]():
                copy.wait()
            start(waited[0] + window)
            waited[0] += 1

    for i in range(window):
        start(i)

    barrier = pltpu.get_barrier_semaphore()

    def greet(d, carry):
        pl.semaphore_signal(
            barrier, inc=1, device_id={"tp": (t + d) % nt}, device_id_type=MESH
        )
        return carry

    lax.fori_loop(1, nt, greet, 0)
    for d in range(1, nr):
        pl.semaphore_signal(
            barrier, inc=1, device_id={"rep": (r + d) % nr}, device_id_type=MESH
        )
    pl.semaphore_signal(barrier, inc=1, device_id={"exp": other}, device_id_type=MESH)

    lane = lax.broadcasted_iota(jnp.int32, (rows, LANES), 1)
    sub = lax.broadcasted_iota(jnp.int32, (rows, LANES), 0)
    weight = jnp.zeros((rows, LANES), jnp.float32)
    for i in range(rows):
        for k in range(ids_ref.shape[0]):
            value = gates_ref[k, i].astype(jnp.float32) * (1.0 / 256.0)
            weight += jnp.where((sub == i) & (lane == ids_ref[k, i]), value, 0.0)
    xg[me, :, :width] = tok_ref[...]
    xg[me, :, width:] = weight.astype(jnp.bfloat16)

    pl.semaphore_wait(barrier, nt + nr - 1)

    def send(slot, send_sem, device):
        return pltpu.make_async_remote_copy(
            src_ref=xg.at[slot], dst_ref=xg.at[slot],
            send_sem=send_sem, recv_sem=g_recv.at[slot],
            device_id=device, device_id_type=MESH,
        )

    def z_copy(d):
        return send(me, zs.at[d], {"tp": ((z + d) % nz) * ny + y})

    def r_copy(slot, i, d):
        return send(slot, rs.at[d, i], {"rep": (r + d) % nr})

    def y_copy(slot, i, d):
        return send(slot, ys.at[d, i], {"tp": z * ny + (y + d) % ny})

    def e_copy(slot):
        return send(slot, es.at[slot % (nr * nt)], {"exp": other})

    def arrived(slot):
        send(slot, zs.at[0], {"exp": other}).wait_recv()

    def pass_y(slot, i):
        def go(d, carry):
            y_copy(slot, i, d).start()
            return carry

        lax.fori_loop(1, ny, go, 0)

    def pass_r(slot, i):
        for d in range(1, nr):
            r_copy(slot, i, d).start()

    def z_start(d, carry):
        z_copy(d).start()
        return carry

    lax.fori_loop(1, nz, z_start, 0)
    pass_r(me, z)
    pass_y(me, r * nz + z)
    e_copy(me).start()

    def z_relay(d, carry):
        zz = (z + nz - d) % nz
        slot = slot_of(e, r, zz * ny + y)
        arrived(slot)
        pass_r(slot, zz)
        pass_y(slot, r * nz + zz)
        e_copy(slot).start()
        return carry

    lax.fori_loop(1, nz, z_relay, 0)
    pump(1)

    def r_relay(i, carry):
        rr = (r + nr - 1 - i // nz) % nr
        zz = (z + nz - i % nz) % nz
        slot = slot_of(e, rr, zz * ny + y)
        arrived(slot)
        pass_y(slot, rr * nz + zz)
        e_copy(slot).start()
        return carry

    lax.fori_loop(0, (nr - 1) * nz, r_relay, 0)
    pump(2)

    def y_relay(i, carry):
        yy = (y + ny - 1 - i // (nr * nz)) % ny
        rr = (r + i // nz) % nr
        zz = (z + nz - i % nz) % nz
        slot = slot_of(e, rr, zz * ny + yy)
        arrived(slot)
        e_copy(slot).start()
        return carry

    lax.fori_loop(0, (ny - 1) * nr * nz, y_relay, 0)
    pump(4)

    def arrive(i, carry):
        arrived(other * nr * nt + i)
        return carry

    lax.fori_loop(0, nr * nt, arrive, 0)

    def lay(g, carry):
        for i in range(group):
            stage[i * rows:(i + 1) * rows, :] = xg[g * group + i].astype(jnp.float32)
        r0 = pl.multiple_of(g * group * rows, group * rows)
        for k in range(nk):
            x[k, pl.ds(r0, group * rows), :] = stage[:, k * kc:(k + 1) * kc].astype(jnp.bfloat16)
        wst[pl.ds(r0, group * rows), :] = stage[:, width:]
        return carry

    lax.fori_loop(0, tokens // (group * rows), lay, 0)

    step = 256
    for l in range(own):
        for k in range(nk):
            pump(l * nk + k + 1)
            for n in range(0, hidden, step):
                cols = slice(n, min(n + step, hidden))
                gate, upper = (
                    jnp.dot(
                        x[k], wbuf[l, m, k * kc:(k + 1) * kc, cols],
                        preferred_element_type=jnp.float32,
                    )
                    for m in range(2)
                )
                if k > 0:
                    gate = gate + acc[0, :, cols]
                    upper = upper + acc[1, :, cols]
                if k < nk - 1:
                    acc[0, :, cols] = gate
                    acc[1, :, cols] = upper
                else:
                    h[l, :, cols] = (gate / (1.0 + jnp.exp(-gate)) * upper).astype(jnp.bfloat16)

    lanes = lax.broadcasted_iota(jnp.int32, (tokens, LANES), 1)
    first = e * experts + r * own
    scales = [
        jnp.sum(jnp.where(lanes == first + l, wst[...], 0.0), axis=1, keepdims=True)
        for l in range(own)
    ]

    def ex_copy(c):
        return pltpu.make_async_remote_copy(
            src_ref=ex_send.at[c], dst_ref=ex_recv.at[c],
            send_sem=ex_ssem.at[c], recv_sem=ex_rsem.at[c],
            device_id={"exp": other}, device_id_type=MESH,
        )

    def rp_copy(c, d):
        target = (r + d) % nr
        return pltpu.make_async_remote_copy(
            src_ref=rp_send.at[c, target], dst_ref=rp_recv.at[c, d],
            send_sem=rp_ssem.at[c, d], recv_sem=rp_rsem.at[c, d],
            device_id={"rep": target}, device_id_type=MESH,
        )

    def tp_copy(c, d):
        target = (t + d) % nt
        return pltpu.make_async_remote_copy(
            src_ref=tp_send.at[c, target], dst_ref=tp_recv.at[c, t],
            send_sem=tp_ssem.at[c, d], recv_sem=tp_rsem.at[c, t],
            device_id={"tp": target}, device_id_type=MESH,
        )

    def tp_from(c, source):
        return pltpu.make_async_remote_copy(
            src_ref=tp_send.at[c, source], dst_ref=tp_recv.at[c, source],
            send_sem=tp_ssem.at[c, 0], recv_sem=tp_rsem.at[c, source],
            device_id={"tp": source}, device_id_type=MESH,
        )

    def down(c):
        pump(own * nk + c + 1)
        for n in range(0, cw, step):
            cols = slice(n, min(n + step, cw))
            total = None
            for l in range(own):
                part = scales[l] * jnp.dot(
                    h[l], dbuf[l, c, :, cols], preferred_element_type=jnp.float32
                )
                total = part if total is None else total + part
            low, high = total[:half], total[half:]
            keep[c, :, cols] = jnp.where(e == 0, low, high)
            ex_send[c, :, cols] = jnp.where(e == 0, high, low).astype(jnp.bfloat16)
        ex_copy(c).start()

    def pass_ex(c):
        ex_copy(c).wait_recv()
        picked = None
        for rr in range(nr):
            span = slice(rr * quarter, (rr + 1) * quarter)
            total = keep[c, span, :] + ex_recv[c, span, :].astype(jnp.float32)
            rp_send[c, rr] = total.astype(jnp.bfloat16)
            picked = total if picked is None else jnp.where(r == rr, total, picked)
        mine[c] = picked
        for d in range(1, nr):
            rp_copy(c, d).start()

    def pass_rp(c):
        total = mine[c]
        for d in range(1, nr):
            rp_copy(c, d).wait_recv()
            total = total + rp_recv[c, d].astype(jnp.float32)
        for j in range(nt):
            tp_send[c, j] = total[j * rows:(j + 1) * rows, :].astype(jnp.bfloat16)
        tp_recv[c, t] = tp_send[c, t]

        def go(d, carry):
            tp_copy(c, d).start()
            return carry

        lax.fori_loop(1, nt, go, 0)

    def collect(c):
        def wait(d, carry):
            tp_from(c, (t + nt - d) % nt).wait_recv()
            return carry

        lax.fori_loop(1, nt, wait, 0)
        total = tp_recv[c, 0].astype(jnp.float32)
        for j in range(1, nt):
            total += tp_recv[c, j].astype(jnp.float32)
        out_ref[:, c * cw:(c + 1) * cw] = total.astype(out_ref.dtype)

    lag_ex, lag_rp = 2, 5
    for c in range(nc):
        down(c)
        if c >= lag_ex:
            pass_ex(c - lag_ex)
        if c >= lag_rp:
            pass_rp(c - lag_rp)
    done_ex, done_rp = max(nc - lag_ex, 0), max(nc - lag_rp, 0)
    while done_rp < nc:
        if done_ex < nc:
            pass_ex(done_ex)
            done_ex += 1
        pass_rp(done_rp)
        done_rp += 1
    for c in range(nc):
        collect(c)

    def z_drain(d, carry):
        z_copy(d).wait_send()
        return carry

    lax.fori_loop(1, nz, z_drain, 0)

    def r_drain(i, carry):
        for d in range(1, nr):
            r_copy(me, i, d).wait_send()
        return carry

    lax.fori_loop(0, nz, r_drain, 0)

    def y_drain(i, carry):
        def inner(d, c):
            y_copy(me, i, d).wait_send()
            return c

        return lax.fori_loop(1, ny, inner, carry)

    lax.fori_loop(0, nr * nz, y_drain, 0)

    def e_drain(i, carry):
        e_copy(e * nr * nt + i).wait_send()
        return carry

    lax.fori_loop(0, nr * nt, e_drain, 0)

    def c_drain(c, carry):
        ex_copy(c).wait_send()
        for d in range(1, nr):
            rp_copy(c, d).wait_send()

        def inner(d, i):
            tp_copy(c, d).wait_send()
            return i

        return lax.fori_loop(1, nt, inner, carry)

    lax.fori_loop(0, nc, c_drain, 0)


def body(tokens, expert_ids, gate_ints, gate_weight, up_weight, down_weight):
    rows, width = tokens.shape
    experts, _, hidden = gate_weight.shape
    nt = lax.axis_size("tp")
    nr = lax.axis_size("rep")
    ny = 1
    while nt % (ny * 2) == 0 and (ny * 2) ** 2 <= nt:
        ny *= 2
    nz = nt // ny
    assert experts % nr == 0 and lax.axis_size("exp") == 2
    own = experts // nr
    slots = nt * nr * 2
    total = slots * rows
    kc = min(512, width)
    cw = min(512, width)
    nk, nc = width // kc, width // cw
    bf16, f32 = jnp.bfloat16, jnp.float32
    vmem = pl.BlockSpec(memory_space=pltpu.VMEM)
    smem = pl.BlockSpec(memory_space=pltpu.SMEM)
    hbm = pl.BlockSpec(memory_space=pl.ANY)
    dma = pltpu.SemaphoreType.DMA
    return pl.pallas_call(
        functools.partial(kernel, (nr, nz, ny, own), kc, cw, 4),
        out_shape=jax.ShapeDtypeStruct((rows, width), bf16),
        in_specs=[smem, smem, vmem, hbm, hbm, hbm],
        out_specs=vmem,
        scratch_shapes=[
            pltpu.VMEM((slots, rows, width + LANES), bf16),
            pltpu.VMEM((16, width + LANES), f32),
            pltpu.VMEM((nk, total, kc), bf16),
            pltpu.VMEM((total, LANES), f32),
            pltpu.VMEM((2, total, hidden), f32),
            pltpu.VMEM((own, total, hidden), bf16),
            pltpu.VMEM((own, 2, width, hidden), bf16),
            pltpu.VMEM((own, nc, hidden, cw), bf16),
            pltpu.VMEM((nc, total // 2, cw), f32),
            pltpu.VMEM((nc, nt * rows, cw), f32),
            pltpu.VMEM((nc, total // 2, cw), bf16),
            pltpu.VMEM((nc, total // 2, cw), bf16),
            pltpu.VMEM((nc, nr, nt * rows, cw), bf16),
            pltpu.VMEM((nc, nr, nt * rows, cw), bf16),
            pltpu.VMEM((nc, nt, rows, cw), bf16),
            pltpu.VMEM((nc, nt, rows, cw), bf16),
            dma((own, 2, nk)),
            dma((own, nc)),
            dma((nz,)),
            dma((nr, nz)),
            dma((ny, nr * nz)),
            dma((nr * nt,)),
            dma((slots,)),
            dma((nc,)),
            dma((nc,)),
            dma((nc, nr)),
            dma((nc, nr)),
            dma((nc, nt)),
            dma((nc, nt)),
        ],
        compiler_params=pltpu.CompilerParams(
            collective_id=0, has_side_effects=True, vmem_limit_bytes=VMEM_BYTES
        ),
    )(expert_ids.T, gate_ints.T, tokens, gate_weight, up_weight, down_weight)


def solution(mesh):
    return jax.shard_map(
        body,
        mesh=mesh,
        in_specs=(
            P(("rep", "exp", "tp"), None),
            P(("rep", "exp", "tp"), None),
            P(("rep", "exp", "tp"), None),
            P("exp", None, "tp"),
            P("exp", None, "tp"),
            P("exp", "tp", None),
        ),
        out_specs=P(("rep", "exp", "tp"), None),
        check_vma=False,
    )
```

time: 45.1 us -> 43.5 us (0.965)
  Pallas kernels: 43.5 us -> 41.9 us
    pallas_call x1, Pallas kernels: 43.5 us -> 41.9 us  [body(): pl.pallas_call(functools.partial(kernel, (nr, nz, ny, own), kc, cw, 4), o...]
where the time goes in v1:
time: 43.5 us; the launch traced here: 43.3 us
  Pallas kernels  41.9 us (96%)
  local copies, waits for them, and re-layouts  1.39 us (3%)
    pallas_call x1, Pallas kernels, body(): pl.pallas_call(functools.partial(kernel, (nr, nz, ny, own), kc, cw, 4), o...  41.9 us
    unnamed x1, local copies, waits for them, and re-layouts  1.39 us

profile of v1, /device:TPU:0, one launch (start us, length us, event | category | flops | bytes accessed | tf_op | source)
XLA Modules:
  0.0 43.3 jit_solution(17584021238801333489)
XLA Ops:
  0.0 41.9 %shard_map.64 = bf16[4,4096]{1,0:T(4,128)(2,1)} custom-call(s32[2,4]{1,0:T(2,128)} %bitcast.2, s32[2,4]{1,0:T(2,128)} %bitcast.3, bf16[4,4096]{1,0:T(4,128)(2,1)} %tok_ref.1, bf16[2,4096,1792]{2,1,0:T(8,128)(2,1)} %gw_ref.1, bf16[2,4096,1792]{2,1,0:T(8,128)(2,1)} %uw_ref.1, bf16[2,1792,4096]{2,1,0:T(8,128)(2,1)} %dw_ref.1), custom_call_target="tpu_custom_call" | custom-call | tf_op jit(solution)/shard_map/pallas_call | solution.py:395
  41.9 1.4 %copy.8 = bf16[4,4096]{1,0:T(4,128)(2,1)} copy(bf16[4,4096]{1,0:T(4,128)(2,1)} %shard_map.64) | data formatting | bytes 65536

commit v2 on v1

v2 whole, which is shorter than its diff:
```python
import functools

import jax
import jax.numpy as jnp
from jax import lax
from jax.experimental import pallas as pl
from jax.experimental.pallas import tpu as pltpu
from jax.sharding import PartitionSpec as P

MESH = pl.DeviceIdType.MESH
LANES = 128
VMEM_BYTES = 67043328
GREET_ALL = False


def kernel(
    dims, kc, cw, pieces, staged,
    ids_hbm, gates_hbm, tok_hbm, gw_ref, uw_ref, dw_ref, out_ref,
    ids_ref, gates_ref, xg, stage, x, wst, acc, h, wbuf, dbuf, keep, mine_a,
    ex_send, ex_recv, a_send, a_recv, b_send, b_recv, f_send, f_recv,
    in_sem, gu_sem, dn_sem, zs, as_, bs, es, g_recv,
    ex_ssem, ex_rsem, a_ssem, a_rsem, b_ssem, b_rsem, f_ssem, f_rsem,
):
    na, nb, nz, ny, own, swap = dims
    r = lax.axis_index("rep")
    e = lax.axis_index("exp")
    t = lax.axis_index("tp")
    z, y = t // ny, t % ny
    other = 1 - e
    turn = e if swap else 0
    a, b = r + turn * (y - r), y + turn * (r - y)
    rows, width = tok_hbm.shape
    hidden = gw_ref.shape[2]
    experts = gw_ref.shape[0]
    nk, tokens, _ = x.shape
    half = tokens // 2
    part_a, part_b = half // na, half // na // nb
    nc = width // cw
    wk = width // pieces
    group = stage.shape[0] // rows
    nab, nf = na * nb * nz, nb * nz

    def slot_of(ee, aa, bb, zz):
        return ((ee * na + aa) * nb + bb) * nz + zz

    def device(aa, bb, zz):
        return {"rep": aa + turn * (bb - aa), "tp": zz * ny + bb + turn * (aa - bb)}

    def near(i):
        m = jnp.minimum(z, nz - 1 - z)
        both = (1 - 2 * ((i + 1) % 2)) * ((i + 1) // 2)
        one = jnp.where(z < nz - 1 - z, 1, -1) * (i - m)
        return z + jnp.where(i <= 2 * m, both, one)

    me = slot_of(e, a, b, z)

    barrier = pltpu.get_barrier_semaphore()
    greeted = 0

    def greet(device_id):
        pl.semaphore_signal(barrier, inc=1, device_id=device_id, device_id_type=MESH)

    for d in range(1, nz):
        greet(device(a, b, (z + d) % nz))
        greeted += 1
    for d in range(1, na):
        greet(device((a + d) % na, b, z))
        greeted += 1
    for d in range(1, nb):
        greet(device(a, (b + d) % nb, z))
        greeted += 1
        if GREET_ALL:
            for i in range(1, nz):
                greet(device(a, (b + d) % nb, (z + i) % nz))
                greeted += 1
    greet({"exp": other})
    greeted += 1

    def load_own():
        copies = [
            pltpu.make_async_copy(
                tok_hbm.at[:, pl.ds(p * wk, wk)], xg.at[p, me, :, pl.ds(0, wk)], in_sem.at[2 + p]
            )
            for p in range(pieces)
        ]
        copies.append(pltpu.make_async_copy(ids_hbm, ids_ref, in_sem.at[0]))
        copies.append(pltpu.make_async_copy(gates_hbm, gates_ref, in_sem.at[1]))
        return copies

    for copy in load_own():
        copy.start()

    def gu_copies(l, k):
        k0 = pl.multiple_of(k * kc, kc)
        return [
            pltpu.make_async_copy(
                ref.at[r * own + l, pl.ds(k0, kc), :],
                wbuf.at[l, m, pl.ds(k0, kc), :],
                gu_sem.at[l, m, k],
            )
            for m, ref in enumerate((gw_ref, uw_ref))
        ]

    def dn_copies(c):
        return [
            pltpu.make_async_copy(
                dw_ref.at[r * own + l, :, pl.ds(c * cw, cw)], dbuf.at[l, c], dn_sem.at[l, c]
            )
            for l in range(own)
        ]

    def gu_start(k, carry):
        for l in range(own):
            for copy in gu_copies(l, k):
                copy.start()
        return carry

    lax.fori_loop(0, nk, gu_start, 0)

    def dn_start(low, high):
        for c in range(low, min(high, nc)):
            for copy in dn_copies(c):
                copy.start()

    acc[...] = jnp.zeros_like(acc)

    for copy in load_own():
        copy.wait()
    lane = lax.broadcasted_iota(jnp.int32, (rows, LANES), 1)
    same = (
        lax.broadcasted_iota(jnp.int32, (rows, rows), 0)
        == lax.broadcasted_iota(jnp.int32, (rows, rows), 1)
    )
    weight = jnp.zeros((rows, LANES), jnp.float32)
    for k in range(ids_ref.shape[0]):
        ids, gates = (
            jnp.sum(
                jnp.where(same, jnp.broadcast_to(ref[k:k + 1, :].astype(jnp.float32), (rows, rows)), 0.0),
                axis=1, keepdims=True,
            )
            for ref in (ids_ref, gates_ref)
        )
        weight += jnp.where(lane.astype(jnp.float32) == ids, gates * (1.0 / 256.0), 0.0)
    xg[pieces - 1, me, :, wk:] = weight.astype(jnp.bfloat16)

    pl.semaphore_wait(barrier, greeted)

    def send(p, slot, send_sem, device_id):
        span = pl.ds(0, wk + LANES if p == pieces - 1 else wk)
        return pltpu.make_async_remote_copy(
            src_ref=xg.at[p, slot, :, span], dst_ref=xg.at[p, slot, :, span],
            send_sem=send_sem, recv_sem=g_recv.at[p, slot],
            device_id=device_id, device_id_type=MESH,
        )

    def z_copy(p, d):
        return send(p, me, zs.at[p, d], device(a, b, (z + d) % nz))

    def a_copy(p, slot, i, d):
        return send(p, slot, as_.at[p, d, i], device((a + d) % na, b, z))

    def b_copy(p, slot, i, d):
        return send(p, slot, bs.at[p, d, i], device(a, (b + d) % nb, z))

    def e_copy(p, slot):
        return send(p, slot, es.at[p, slot % nab], {"exp": other})

    def arrived(p, slot):
        send(p, slot, zs.at[p, 0], {"exp": other}).wait_recv()

    def pass_on(p, slot, i_a, i_b):
        if i_b is not None:
            for d in range(1, nb):
                b_copy(p, slot, i_b, d).start()
        if i_a is not None:
            for d in range(1, na):
                a_copy(p, slot, i_a, d).start()
        e_copy(p, slot).start()

    for p in range(pieces):
        for d in range(1, nz):
            z_copy(p, d).start()
        pass_on(p, me, z, a * nz + z)

    def z_relay(p):
        def go(i, carry):
            zz = near(i)
            slot = slot_of(e, a, b, zz)
            arrived(p, slot)
            pass_on(p, slot, zz, a * nz + zz)
            return carry

        lax.fori_loop(1, nz, go, 0)

    def a_relay(p):
        def go(i, carry):
            aa = (a + 1 + i // nz) % na
            zz = jnp.where(i % nz == 0, z, near(i % nz))
            slot = slot_of(e, aa, b, zz)
            arrived(p, slot)
            pass_on(p, slot, None, aa * nz + zz)
            return carry

        lax.fori_loop(0, (na - 1) * nz, go, 0)

    def b_relay(p):
        def go(i, carry):
            bb = (b + 1 + i // (na * nz)) % nb
            aa = (a + i // nz) % na
            zz = jnp.where(i % nz == 0, z, near(i % nz))
            slot = slot_of(e, aa, bb, zz)
            arrived(p, slot)
            pass_on(p, slot, None, None)
            return carry

        lax.fori_loop(0, (nb - 1) * na * nz, go, 0)

    def e_arrive(p):
        def go(i, carry):
            arrived(p, other * nab + i)
            return carry

        lax.fori_loop(0, nab, go, 0)

    nkp = nk // pieces

    def lay(p, side):
        def go(g, carry):
            slot = side * nab + g * group
            for i in range(group):
                stage[i * rows:(i + 1) * rows, :] = xg[p, slot + i].astype(jnp.float32)
            r0 = pl.multiple_of(slot * rows, group * rows)
            for k in range(nkp):
                x[p * nkp + k, pl.ds(r0, group * rows), :] = (
                    stage[:, k * kc:(k + 1) * kc].astype(jnp.bfloat16)
                )
            if p == pieces - 1:
                wst[pl.ds(r0, group * rows), :] = stage[:, wk:]
            return carry

        lax.fori_loop(0, half // (group * rows), go, 0)

    for p in range(pieces):
        z_relay(p)
    for p in range(pieces):
        a_relay(p)
    dn_start(0, 3)
    for p in range(pieces):
        b_relay(p)
    dn_start(3, nc)

    step = 256

    def dots(l, k, cols):
        k0 = pl.multiple_of(k * kc, kc)
        return (
            jnp.dot(x[k], wbuf[l, m, pl.ds(k0, kc), cols], preferred_element_type=jnp.float32)
            + acc[l, m, :, cols]
            for m in range(2)
        )

    def gu_step(k, carry):
        for l in range(own):
            for copy in gu_copies(l, k):
                copy.wait()
            for n in range(0, hidden, step):
                cols = slice(n, min(n + step, hidden))
                for m, value in enumerate(dots(l, k, cols)):
                    acc[l, m, :, cols] = value
        return carry

    def gu_last(k):
        for l in range(own):
            for copy in gu_copies(l, k):
                copy.wait()
            for n in range(0, hidden, step):
                cols = slice(n, min(n + step, hidden))
                gate, upper = dots(l, k, cols)
                h[l, :, cols] = (gate / (1.0 + jnp.exp(-gate)) * upper).astype(jnp.bfloat16)

    for p in range(pieces):
        lay(p, e)
        e_arrive(p)
        lay(p, other)
        last = p == pieces - 1
        lax.fori_loop(p * nkp, (p + 1) * nkp - (1 if last else 0), gu_step, 0)
    gu_last(nk - 1)

    lanes = lax.broadcasted_iota(jnp.int32, (tokens, LANES), 1)
    first = e * experts + r * own
    scales = [
        jnp.sum(jnp.where(lanes == first + l, wst[...], 0.0), axis=1, keepdims=True)
        for l in range(own)
    ]

    def ex_copy(c):
        return pltpu.make_async_remote_copy(
            src_ref=ex_send.at[c], dst_ref=ex_recv.at[c],
            send_sem=ex_ssem.at[c], recv_sem=ex_rsem.at[c],
            device_id={"exp": other}, device_id_type=MESH,
        )

    def sa_copy(c, d):
        target = (a + d) % na
        return pltpu.make_async_remote_copy(
            src_ref=a_send.at[c, target], dst_ref=a_recv.at[c, d],
            send_sem=a_ssem.at[c, d], recv_sem=a_rsem.at[c, d],
            device_id=device(target, b, z), device_id_type=MESH,
        )

    def sb_copy(c, d):
        target = (b + d) % nb
        return pltpu.make_async_remote_copy(
            src_ref=b_send.at[c, target], dst_ref=b_recv.at[c, d],
            send_sem=b_ssem.at[c, d], recv_sem=b_rsem.at[c, d],
            device_id=device(a, target, z), device_id_type=MESH,
        )

    def f_copy(c, d):
        if staged[c]:
            mine, target = z, (z + d) % nz
            where = device(a, b, target)
        else:
            mine = b * nz + z
            target = (mine + d) % nf
            where = device(a, target // nz, target % nz)
        return pltpu.make_async_remote_copy(
            src_ref=f_send.at[c, target], dst_ref=f_recv.at[c, mine],
            send_sem=f_ssem.at[c, d], recv_sem=f_rsem.at[c, mine],
            device_id=where, device_id_type=MESH,
        )

    def f_from(c, source):
        return pltpu.make_async_remote_copy(
            src_ref=f_send.at[c, source], dst_ref=f_recv.at[c, source],
            send_sem=f_ssem.at[c, 0], recv_sem=f_rsem.at[c, source],
            device_id={"exp": other}, device_id_type=MESH,
        )

    def down(c):
        for copy in dn_copies(c):
            copy.wait()
        for n in range(0, cw, step):
            cols = slice(n, min(n + step, cw))
            total = None
            for l in range(own):
                part = scales[l] * jnp.dot(
                    h[l], dbuf[l, c, :, cols], preferred_element_type=jnp.float32
                )
                total = part if total is None else total + part
            low, high = total[:half], total[half:]
            keep[c, :, cols] = jnp.where(e == 0, low, high)
            ex_send[c, :, cols] = jnp.where(e == 0, high, low).astype(jnp.bfloat16)
        ex_copy(c).start()

    def pass_ex(c):
        ex_copy(c).wait_recv()
        picked = None
        for aa in range(na):
            span = slice(aa * part_a, (aa + 1) * part_a)
            total = keep[c, span, :] + ex_recv[c, span, :].astype(jnp.float32)
            a_send[c, aa] = total.astype(jnp.bfloat16)
            picked = total if picked is None else jnp.where(a == aa, total, picked)
        mine_a[c] = picked
        for d in range(1, na):
            sa_copy(c, d).start()

    def send_final(c, total, count, mine):
        for j in range(count):
            f_send[c, j] = total[j * rows:(j + 1) * rows, :].astype(jnp.bfloat16)
        f_recv[c, mine] = f_send[c, mine]

        def go(d, carry):
            f_copy(c, d).start()
            return carry

        lax.fori_loop(1, count, go, 0)

    def pass_a(c):
        total = mine_a[c]
        for d in range(1, na):
            sa_copy(c, d).wait_recv()
            total = total + a_recv[c, d].astype(jnp.float32)
        if not staged[c]:
            send_final(c, total, nf, b * nz + z)
            return
        picked = None
        for bb in range(nb):
            span = total[bb * part_b:(bb + 1) * part_b]
            b_send[c, bb] = span.astype(jnp.bfloat16)
            picked = span if picked is None else jnp.where(b == bb, span, picked)
        keep[c, 0:part_b, :] = picked
        for d in range(1, nb):
            sb_copy(c, d).start()

    def pass_b(c):
        if not staged[c]:
            return
        total = keep[c, 0:part_b, :]
        for d in range(1, nb):
            sb_copy(c, d).wait_recv()
            total = total + b_recv[c, d].astype(jnp.float32)
        send_final(c, total, nz, z)

    def collect(c):
        count, mine = (nz, z) if staged[c] else (nf, b * nz + z)

        def wait(d, carry):
            f_from(c, (mine + count - d) % count).wait_recv()
            return carry

        lax.fori_loop(1, count, wait, 0)
        total = f_recv[c, 0].astype(jnp.float32)
        for j in range(1, count):
            total += f_recv[c, j].astype(jnp.float32)
        out_ref[:, c * cw:(c + 1) * cw] = total.astype(out_ref.dtype)

    def gather_drain():
        for p in range(pieces):
            for d in range(1, nz):
                z_copy(p, d).wait_send()

            def a_drain(i, carry, p=p):
                for d in range(1, na):
                    a_copy(p, me, i, d).wait_send()
                return carry

            lax.fori_loop(0, nz, a_drain, 0)

            def b_drain(i, carry, p=p):
                for d in range(1, nb):
                    b_copy(p, me, i, d).wait_send()
                return carry

            lax.fori_loop(0, na * nz, b_drain, 0)

            def e_drain(i, carry, p=p):
                e_copy(p, e * nab + i).wait_send()
                return carry

            lax.fori_loop(0, nab, e_drain, 0)

    def sum_drain(c):
        ex_copy(c).wait_send()
        for d in range(1, na):
            sa_copy(c, d).wait_send()
        if staged[c]:
            for d in range(1, nb):
                sb_copy(c, d).wait_send()

        def inner(d, carry):
            f_copy(c, d).wait_send()
            return carry

        lax.fori_loop(1, nz if staged[c] else nf, inner, 0)

    lag_ex, lag_b = 2, 3
    for c in range(nc + lag_ex):
        if c < nc:
            down(c)
        if c >= lag_ex:
            pass_ex(c - lag_ex)
    gather_drain()
    for c in range(nc + lag_b):
        if c < nc:
            pass_a(c)
        if c >= lag_b:
            pass_b(c - lag_b)
    for c in range(nc):
        sum_drain(c)
    for c in range(nc):
        collect(c)


def body(tokens, expert_ids, gate_ints, gate_weight, up_weight, down_weight):
    rows, width = tokens.shape
    experts, _, hidden = gate_weight.shape
    nt = lax.axis_size("tp")
    nr = lax.axis_size("rep")
    ny = 1
    while nt % (ny * 2) == 0 and (ny * 2) ** 2 <= nt:
        ny *= 2
    nz = nt // ny
    assert experts % nr == 0 and lax.axis_size("exp") == 2
    own = experts // nr
    slots = nt * nr * 2
    total = slots * rows
    pieces = 2
    kc = min(512, width // pieces)
    cw = min(512, width)
    nk, nc = width // kc, width // cw
    swap = nr == ny
    staged = tuple(c < nc // 2 for c in range(nc))
    bf16, f32, i32 = jnp.bfloat16, jnp.float32, jnp.int32
    vmem = pl.BlockSpec(memory_space=pltpu.VMEM)
    hbm = pl.BlockSpec(memory_space=pl.ANY)
    dma = pltpu.SemaphoreType.DMA
    part_a = total // 2 // nr
    part_b = part_a // ny
    top = expert_ids.shape[1]
    return pl.pallas_call(
        functools.partial(kernel, (nr, ny, nz, ny, own, swap), kc, cw, pieces, staged),
        out_shape=jax.ShapeDtypeStruct((rows, width), bf16),
        in_specs=[hbm] * 6,
        out_specs=vmem,
        scratch_shapes=[
            pltpu.VMEM((top, rows), i32),
            pltpu.VMEM((top, rows), i32),
            pltpu.VMEM((pieces, slots, rows, width // pieces + LANES), bf16),
            pltpu.VMEM((16, width // pieces + LANES), f32),
            pltpu.VMEM((nk, total, kc), bf16),
            pltpu.VMEM((total, LANES), f32),
            pltpu.VMEM((own, 2, total, hidden), f32),
            pltpu.VMEM((own, total, hidden), bf16),
            pltpu.VMEM((own, 2, width, hidden), bf16),
            pltpu.VMEM((own, nc, hidden, cw), bf16),
            pltpu.VMEM((nc, total // 2, cw), f32),
            pltpu.VMEM((nc, part_a, cw), f32),
            pltpu.VMEM((nc, total // 2, cw), bf16),
            pltpu.VMEM((nc, total // 2, cw), bf16),
            pltpu.VMEM((nc, nr, part_a, cw), bf16),
            pltpu.VMEM((nc, nr, part_a, cw), bf16),
            pltpu.VMEM((nc, ny, part_b, cw), bf16),
            pltpu.VMEM((nc, ny, part_b, cw), bf16),
            pltpu.VMEM((nc, nt, rows, cw), bf16),
            pltpu.VMEM((nc, nt, rows, cw), bf16),
            dma((2 + pieces,)),
            dma((own, 2, nk)),
            dma((own, nc)),
            dma((pieces, nz)),
            dma((pieces, nr, nz)),
            dma((pieces, ny, nr * nz)),
            dma((pieces, nr * nt)),
            dma((pieces, slots)),
            dma((nc,)),
            dma((nc,)),
            dma((nc, nr)),
            dma((nc, nr)),
            dma((nc, ny)),
            dma((nc, ny)),
            dma((nc, nt)),
            dma((nc, nt)),
        ],
        compiler_params=pltpu.CompilerParams(
            collective_id=0, has_side_effects=True, vmem_limit_bytes=VMEM_BYTES
        ),
    )(expert_ids.T, gate_ints.T, tokens, gate_weight, up_weight, down_weight)


def solution(mesh):
    return jax.shard_map(
        body,
        mesh=mesh,
        in_specs=(
            P(("rep", "exp", "tp"), None),
            P(("rep", "exp", "tp"), None),
            P(("rep", "exp", "tp"), None),
            P("exp", None, "tp"),
            P("exp", None, "tp"),
            P("exp", "tp", None),
        ),
        out_specs=P(("rep", "exp", "tp"), None),
        check_vma=False,
    )
```

time: 43.5 us -> 42.1 us (0.968)
  Pallas kernels: 41.9 us -> 40.5 us
    pallas_call x1, Pallas kernels: 41.9 us -> 40.5 us  [body(): pl.pallas_call(functools.partial(kernel, (nr, ny, nz, ny, own, swap), kc,...]
where the time goes in v2:
time: 42.1 us; the launch traced here: 41.8 us
  Pallas kernels  40.5 us (96%)
  local copies, waits for them, and re-layouts  1.39 us (3%)
    pallas_call x1, Pallas kernels, body(): pl.pallas_call(functools.partial(kernel, (nr, ny, nz, ny, own, swap), kc,...  40.5 us
    unnamed x1, local copies, waits for them, and re-layouts  1.39 us

profile of v2, /device:TPU:0, one launch (start us, length us, event | category | flops | bytes accessed | tf_op | source)
XLA Modules:
  0.0 41.8 jit_solution(16380086975044787286)
XLA Ops:
  0.0 40.5 %shard_map.64 = bf16[4,4096]{1,0:T(4,128)(2,1)} custom-call(s32[2,4]{1,0:T(2,128)} %bitcast.2, s32[2,4]{1,0:T(2,128)} %bitcast.3, bf16[4,4096]{1,0:T(4,128)(2,1)} %tok_hbm.1, bf16[2,4096,1792]{2,1,0:T(8,128)(2,1)} %gw_ref.1, bf16[2,4096,1792]{2,1,0:T(8,128)(2,1)} %uw_ref.1, bf16[2,1792,4096]{2,1,0:T(8,128)(2,1)} %dw_ref.1), custom_call_target="tpu_custom_call" | custom-call | tf_op jit(solution)/shard_map/pallas_call | solution.py:501
  40.5 1.4 %copy.8 = bf16[4,4096]{1,0:T(4,128)(2,1)} copy(bf16[4,4096]{1,0:T(4,128)(2,1)} %shard_map.64) | data formatting | bytes 65536

commit v3 on v2

v3 whole, which is shorter than its diff:
```python
import functools

import jax
import jax.numpy as jnp
from jax import lax
from jax.experimental import pallas as pl
from jax.experimental.pallas import tpu as pltpu
from jax.sharding import PartitionSpec as P

MESH = pl.DeviceIdType.MESH
LANES = 128
VMEM_BYTES = 67043328


def kernel(
    dims, kc, cw, pieces,
    ids_hbm, gates_hbm, tok_hbm, gw_ref, uw_ref, dw_ref, out_ref,
    ids_ref, gates_ref, xg, stage, x, wst, acc, h, wbuf, dbuf, keep, mine_q,
    ex_send, ex_recv, q_send, q_recv, f_send, f_recv,
    in_sem, gu_sem, dn_sem, zs, qs, es, g_recv,
    ex_ssem, ex_rsem, q_ssem, q_rsem, f_ssem, f_rsem,
):
    nr, ny, nz, own = dims
    nq = nr * ny
    r = lax.axis_index("rep")
    e = lax.axis_index("exp")
    t = lax.axis_index("tp")
    z, q = t // ny, r * ny + t % ny
    other = 1 - e
    rows, width = tok_hbm.shape
    hidden = gw_ref.shape[2]
    experts = gw_ref.shape[0]
    tokens = x.shape[1]
    half = tokens // 2
    part = half // nq
    nk, nc = width // kc, width // cw
    wk = width // pieces
    group = stage.shape[0] // rows
    nqz = nq * nz

    def slot_of(ee, qq, zz):
        return (ee * nq + qq) * nz + zz

    def device(qq, zz):
        return {"rep": qq // ny, "tp": zz * ny + qq % ny}

    def near(i):
        m = jnp.minimum(z, nz - 1 - z)
        both = (1 - 2 * ((i + 1) % 2)) * ((i + 1) // 2)
        one = jnp.where(z < nz - 1 - z, 1, -1) * (i - m)
        return z + jnp.where(i <= 2 * m, both, one)

    me = slot_of(e, q, z)

    barrier = pltpu.get_barrier_semaphore()
    greeted = 0

    def greet(device_id):
        pl.semaphore_signal(barrier, inc=1, device_id=device_id, device_id_type=MESH)

    for d in range(1, nz):
        greet(device(q, (z + d) % nz))
        greeted += 1
    for d in range(1, nq):
        greet(device((q + d) % nq, z))
        greeted += 1
    greet({"exp": other})
    greeted += 1

    def load_own():
        copies = [
            pltpu.make_async_copy(
                tok_hbm.at[:, pl.ds(p * wk, wk)], xg.at[p, me, :, pl.ds(0, wk)], in_sem.at[2 + p]
            )
            for p in range(pieces)
        ]
        copies.append(pltpu.make_async_copy(ids_hbm, ids_ref, in_sem.at[0]))
        copies.append(pltpu.make_async_copy(gates_hbm, gates_ref, in_sem.at[1]))
        return copies

    for copy in load_own():
        copy.start()

    def gu_copies(l, k):
        k0 = pl.multiple_of(k * kc, kc)
        return [
            pltpu.make_async_copy(
                ref.at[r * own + l, pl.ds(k0, kc), :],
                wbuf.at[l, m, pl.ds(k0, kc), :],
                gu_sem.at[l, m, k],
            )
            for m, ref in enumerate((gw_ref, uw_ref))
        ]

    def dn_copies(c):
        return [
            pltpu.make_async_copy(
                dw_ref.at[r * own + l, :, pl.ds(c * cw, cw)], dbuf.at[l, c], dn_sem.at[l, c]
            )
            for l in range(own)
        ]

    def gu_start(k, carry):
        for l in range(own):
            for copy in gu_copies(l, k):
                copy.start()
        return carry

    lax.fori_loop(0, nk, gu_start, 0)

    def dn_start(low, high):
        for c in range(low, min(high, nc)):
            for copy in dn_copies(c):
                copy.start()

    for copy in load_own():
        copy.wait()
    lane = lax.broadcasted_iota(jnp.int32, (rows, LANES), 1)
    same = (
        lax.broadcasted_iota(jnp.int32, (rows, rows), 0)
        == lax.broadcasted_iota(jnp.int32, (rows, rows), 1)
    )
    weight = jnp.zeros((rows, LANES), jnp.float32)
    for k in range(ids_ref.shape[0]):
        ids, gates = (
            jnp.sum(
                jnp.where(same, jnp.broadcast_to(ref[k:k + 1, :].astype(jnp.float32), (rows, rows)), 0.0),
                axis=1, keepdims=True,
            )
            for ref in (ids_ref, gates_ref)
        )
        weight += jnp.where(lane.astype(jnp.float32) == ids, gates * (1.0 / 256.0), 0.0)
    xg[pieces - 1, me, :, wk:] = weight.astype(jnp.bfloat16)

    pl.semaphore_wait(barrier, greeted)

    def send(p, slot, send_sem, device_id):
        span = pl.ds(0, wk + LANES if p == pieces - 1 else wk)
        return pltpu.make_async_remote_copy(
            src_ref=xg.at[p, slot, :, span], dst_ref=xg.at[p, slot, :, span],
            send_sem=send_sem, recv_sem=g_recv.at[p, slot],
            device_id=device_id, device_id_type=MESH,
        )

    def z_copy(p, d):
        return send(p, me, zs.at[p, d], device(q, (z + d) % nz))

    def q_copy(p, slot, i, d):
        return send(p, slot, qs.at[p, d, i], device((q + d) % nq, z))

    def e_copy(p, slot):
        return send(p, slot, es.at[p, slot % nqz], {"exp": other})

    def arrived(p, slot):
        send(p, slot, zs.at[p, 0], {"exp": other}).wait_recv()

    def pass_q(p, slot, i):
        for d in range(1, nq):
            q_copy(p, slot, i, d).start()
        e_copy(p, slot).start()

    for p in range(pieces):
        for d in range(1, nz):
            z_copy(p, d).start()
        pass_q(p, me, z)

    def z_relay(p):
        def go(i, carry):
            zz = near(i)
            slot = slot_of(e, q, zz)
            arrived(p, slot)
            pass_q(p, slot, zz)
            return carry

        lax.fori_loop(1, nz, go, 0)

    def q_relay(p):
        def go(i, carry):
            zz = jnp.where(i // (nq - 1) == 0, z, near(i // (nq - 1)))
            slot = slot_of(e, (q + 1 + i % (nq - 1)) % nq, zz)
            arrived(p, slot)
            e_copy(p, slot).start()
            return carry

        lax.fori_loop(0, (nq - 1) * nz, go, 0)

    def e_arrive(p):
        def go(i, carry):
            arrived(p, other * nqz + i)
            return carry

        lax.fori_loop(0, nqz, go, 0)

    def lay(p, side):
        def go(g, carry):
            slot = side * nqz + g * group
            for i in range(group):
                stage[i * rows:(i + 1) * rows, :] = xg[p, slot + i].astype(jnp.float32)
            r0 = pl.multiple_of(slot * rows, group * rows)
            x[p, pl.ds(r0, group * rows), :] = stage[:, :wk].astype(jnp.bfloat16)
            if p == pieces - 1:
                wst[pl.ds(r0, group * rows), :] = stage[:, wk:]
            return carry

        lax.fori_loop(0, half // (group * rows), go, 0)

    step = 256

    def project(p):
        for l in range(own):
            for k in range(p * nk // pieces, (p + 1) * nk // pieces):
                for copy in gu_copies(l, k):
                    copy.wait()
            for n in range(0, hidden, step):
                cols = slice(n, min(n + step, hidden))
                gate, upper = (
                    jnp.dot(
                        x[p], wbuf[l, m, p * wk:(p + 1) * wk, cols],
                        preferred_element_type=jnp.float32,
                    )
                    for m in range(2)
                )
                if p > 0:
                    gate = gate + acc[l, 0, :, cols]
                    upper = upper + acc[l, 1, :, cols]
                if p < pieces - 1:
                    acc[l, 0, :, cols] = gate
                    acc[l, 1, :, cols] = upper
                else:
                    h[l, :, cols] = (gate / (1.0 + jnp.exp(-gate)) * upper).astype(jnp.bfloat16)

    for p in range(pieces):
        z_relay(p)
    dn_start(0, 3)
    for p in range(pieces):
        q_relay(p)
        if p == 0:
            dn_start(3, nc)
            lay(p, e)
    for p in range(pieces):
        if p > 0:
            lay(p, e)
        e_arrive(p)
        lay(p, other)
        project(p)

    lanes = lax.broadcasted_iota(jnp.int32, (tokens, LANES), 1)
    first = e * experts + r * own
    scales = [
        jnp.sum(jnp.where(lanes == first + l, wst[...], 0.0), axis=1, keepdims=True)
        for l in range(own)
    ]

    def ex_copy(c):
        return pltpu.make_async_remote_copy(
            src_ref=ex_send.at[c], dst_ref=ex_recv.at[c],
            send_sem=ex_ssem.at[c], recv_sem=ex_rsem.at[c],
            device_id={"exp": other}, device_id_type=MESH,
        )

    def sq_copy(c, d):
        target = (q + d) % nq
        return pltpu.make_async_remote_copy(
            src_ref=q_send.at[c, target], dst_ref=q_recv.at[c, d],
            send_sem=q_ssem.at[c, d], recv_sem=q_rsem.at[c, d],
            device_id=device(target, z), device_id_type=MESH,
        )

    def f_copy(c, d):
        target = (z + d) % nz
        return pltpu.make_async_remote_copy(
            src_ref=f_send.at[c, target], dst_ref=f_recv.at[c, d],
            send_sem=f_ssem.at[c, d], recv_sem=f_rsem.at[c, d],
            device_id=device(q, target), device_id_type=MESH,
        )

    def down(c):
        for copy in dn_copies(c):
            copy.wait()
        for n in range(0, cw, step):
            cols = slice(n, min(n + step, cw))
            total = None
            for l in range(own):
                value = scales[l] * jnp.dot(
                    h[l], dbuf[l, c, :, cols], preferred_element_type=jnp.float32
                )
                total = value if total is None else total + value
            low, high = total[:half], total[half:]
            keep[c, :, cols] = jnp.where(e == 0, low, high)
            ex_send[c, :, cols] = jnp.where(e == 0, high, low).astype(jnp.bfloat16)
        ex_copy(c).start()

    def pass_ex(c):
        ex_copy(c).wait_recv()
        picked = None
        for qq in range(nq):
            span = slice(qq * part, (qq + 1) * part)
            total = keep[c, span, :] + ex_recv[c, span, :].astype(jnp.float32)
            q_send[c, qq] = total.astype(jnp.bfloat16)
            picked = total if picked is None else jnp.where(q == qq, total, picked)
        mine_q[c] = picked
        for d in range(1, nq):
            sq_copy(c, d).start()

    def pass_q_sum(c):
        total = mine_q[c]
        for d in range(1, nq):
            sq_copy(c, d).wait_recv()
            total = total + q_recv[c, d].astype(jnp.float32)
        for j in range(nz):
            f_send[c, j] = total[j * rows:(j + 1) * rows, :].astype(jnp.bfloat16)
        f_recv[c, 0] = f_send[c, z]
        for d in range(1, nz):
            f_copy(c, d).start()

    def collect(c):
        for d in range(1, nz):
            f_copy(c, d).wait_recv()
        total = f_recv[c, 0].astype(jnp.float32)
        for d in range(1, nz):
            total += f_recv[c, d].astype(jnp.float32)
        out_ref[:, c * cw:(c + 1) * cw] = total.astype(out_ref.dtype)

    def gather_drain():
        for p in range(pieces):
            for d in range(1, nz):
                z_copy(p, d).wait_send()

            def q_drain(i, carry, p=p):
                for d in range(1, nq):
                    q_copy(p, me, i, d).wait_send()
                return carry

            lax.fori_loop(0, nz, q_drain, 0)

            def e_drain(i, carry, p=p):
                e_copy(p, e * nqz + i).wait_send()
                return carry

            lax.fori_loop(0, nqz, e_drain, 0)

    def sum_drain(c):
        ex_copy(c).wait_send()
        for d in range(1, nq):
            sq_copy(c, d).wait_send()
        for d in range(1, nz):
            f_copy(c, d).wait_send()

    lag_ex, lag_q = 2, 6
    for c in range(nc + lag_q):
        if c < nc:
            down(c)
        if lag_ex <= c < nc + lag_ex:
            pass_ex(c - lag_ex)
        if c == nc:
            gather_drain()
        if c >= lag_q:
            pass_q_sum(c - lag_q)
    for c in range(nc):
        collect(c)
    for c in range(nc):
        sum_drain(c)


def body(tokens, expert_ids, gate_ints, gate_weight, up_weight, down_weight):
    rows, width = tokens.shape
    experts, _, hidden = gate_weight.shape
    nt = lax.axis_size("tp")
    nr = lax.axis_size("rep")
    ny = 1
    while nt % (ny * 2) == 0 and (ny * 2) ** 2 <= nt:
        ny *= 2
    nz = nt // ny
    assert experts % nr == 0 and lax.axis_size("exp") == 2
    own = experts // nr
    slots = nt * nr * 2
    total = slots * rows
    pieces = 2
    kc = min(512, width // pieces)
    cw = min(512, width)
    nk, nc = width // kc, width // cw
    bf16, f32, i32 = jnp.bfloat16, jnp.float32, jnp.int32
    vmem = pl.BlockSpec(memory_space=pltpu.VMEM)
    hbm = pl.BlockSpec(memory_space=pl.ANY)
    dma = pltpu.SemaphoreType.DMA
    nq = nr * ny
    part = total // 2 // nq
    top = expert_ids.shape[1]
    return pl.pallas_call(
        functools.partial(kernel, (nr, ny, nz, own), kc, cw, pieces),
        out_shape=jax.ShapeDtypeStruct((rows, width), bf16),
        in_specs=[hbm] * 6,
        out_specs=vmem,
        scratch_shapes=[
            pltpu.VMEM((top, rows), i32),
            pltpu.VMEM((top, rows), i32),
            pltpu.VMEM((pieces, slots, rows, width // pieces + LANES), bf16),
            pltpu.VMEM((16, width // pieces + LANES), f32),
            pltpu.VMEM((pieces, total, width // pieces), bf16),
            pltpu.VMEM((total, LANES), f32),
            pltpu.VMEM((own, 2, total, hidden), f32),
            pltpu.VMEM((own, total, hidden), bf16),
            pltpu.VMEM((own, 2, width, hidden), bf16),
            pltpu.VMEM((own, nc, hidden, cw), bf16),
            pltpu.VMEM((nc, total // 2, cw), f32),
            pltpu.VMEM((nc, part, cw), f32),
            pltpu.VMEM((nc, total // 2, cw), bf16),
            pltpu.VMEM((nc, total // 2, cw), bf16),
            pltpu.VMEM((nc, nq, part, cw), bf16),
            pltpu.VMEM((nc, nq, part, cw), bf16),
            pltpu.VMEM((nc, nz, rows, cw), bf16),
            pltpu.VMEM((nc, nz, rows, cw), bf16),
            dma((2 + pieces,)),
            dma((own, 2, nk)),
            dma((own, nc)),
            dma((pieces, nz)),
            dma((pieces, nq, nz)),
            dma((pieces, nq * nz)),
            dma((pieces, slots)),
            dma((nc,)),
            dma((nc,)),
            dma((nc, nq)),
            dma((nc, nq)),
            dma((nc, nz)),
            dma((nc, nz)),
        ],
        compiler_params=pltpu.CompilerParams(
            collective_id=0, has_side_effects=True, vmem_limit_bytes=VMEM_BYTES
        ),
    )(expert_ids.T, gate_ints.T, tokens, gate_weight, up_weight, down_weight)


def solution(mesh):
    return jax.shard_map(
        body,
        mesh=mesh,
        in_specs=(
            P(("rep", "exp", "tp"), None),
            P(("rep", "exp", "tp"), None),
            P(("rep", "exp", "tp"), None),
            P("exp", None, "tp"),
            P("exp", None, "tp"),
            P("exp", "tp", None),
        ),
        out_specs=P(("rep", "exp", "tp"), None),
        check_vma=False,
    )
```

time: 42.1 us -> 37.3 us (0.89)
  Pallas kernels: 40.5 us -> 35.7 us
    pallas_call x1, Pallas kernels: 40.5 us -> 35.7 us  [body(): pl.pallas_call(functools.partial(kernel, (nr, ny, nz, own), kc, cw, piece...]
where the time goes in v3:
time: 37.3 us; the launch traced here: 37.1 us
  Pallas kernels  35.7 us (96%)
  local copies, waits for them, and re-layouts  1.39 us (4%)
    pallas_call x1, Pallas kernels, body(): pl.pallas_call(functools.partial(kernel, (nr, ny, nz, own), kc, cw, piece...  35.7 us
    unnamed x1, local copies, waits for them, and re-layouts  1.39 us

profile of v3, /device:TPU:0, one launch (start us, length us, event | category | flops | bytes accessed | tf_op | source)
XLA Modules:
  0.0 37.1 jit_solution(8264873374982389442)
XLA Ops:
  0.0 35.7 %shard_map.64 = bf16[4,4096]{1,0:T(4,128)(2,1)} custom-call(s32[2,4]{1,0:T(2,128)} %bitcast.2, s32[2,4]{1,0:T(2,128)} %bitcast.3, bf16[4,4096]{1,0:T(4,128)(2,1)} %tok_hbm.1, bf16[2,4096,1792]{2,1,0:T(8,128)(2,1)} %gw_ref.1, bf16[2,4096,1792]{2,1,0:T(8,128)(2,1)} %uw_ref.1, bf16[2,1792,4096]{2,1,0:T(8,128)(2,1)} %dw_ref.1), custom_call_target="tpu_custom_call" | custom-call | tf_op jit(solution)/shard_map/pallas_call | solution.py:389
  35.7 1.4 %copy.8 = bf16[4,4096]{1,0:T(4,128)(2,1)} copy(bf16[4,4096]{1,0:T(4,128)(2,1)} %shard_map.64) | data formatting | bytes 65536

commit v4 on v3

--- a/solution.py
+++ b/solution.py
@@ -9,16 +9,16 @@
 
 MESH = pl.DeviceIdType.MESH
 LANES = 128
-VMEM_BYTES = 67043328
+VMEM_BYTES = 62000000
 
 
 def kernel(
-    dims, kc, cw, pieces,
+    dims, cw, pieces,
     ids_hbm, gates_hbm, tok_hbm, gw_ref, uw_ref, dw_ref, out_ref,
     ids_ref, gates_ref, xg, stage, x, wst, acc, h, wbuf, dbuf, keep, mine_q,
     ex_send, ex_recv, q_send, q_recv, f_send, f_recv,
-    in_sem, gu_sem, dn_sem, zs, qs, es, g_recv,
-    ex_ssem, ex_rsem, q_ssem, q_rsem, f_ssem, f_rsem,
+    in_sem, gu_sem, dn_sem, g_send, z_recv, g_recv, e_recv,
+    s_send, ex_rsem, q_rsem, f_rsem,
 ):
     nr, ny, nz, own = dims
     nq = nr * ny
@@ -33,13 +33,13 @@
     tokens = x.shape[1]
     half = tokens // 2
     part = half // nq
-    nk, nc = width // kc, width // cw
+    nc = width // cw
     wk = width // pieces
     group = stage.shape[0] // rows
     nqz = nq * nz
 
     def slot_of(ee, qq, zz):
-        return (ee * nq + qq) * nz + zz
+        return (ee * nz + zz) * nq + qq
 
     def device(qq, zz):
         return {"rep": qq // ny, "tp": zz * ny + qq % ny}
@@ -81,14 +81,14 @@
     for copy in load_own():
         copy.start()
 
-    def gu_copies(l, k):
-        k0 = pl.multiple_of(k * kc, kc)
+    def gu_copies(p):
         return [
             pltpu.make_async_copy(
-                ref.at[r * own + l, pl.ds(k0, kc), :],
-                wbuf.at[l, m, pl.ds(k0, kc), :],
-                gu_sem.at[l, m, k],
+                ref.at[r * own + l, pl.ds(p * wk, wk), :],
+                wbuf.at[l, m, pl.ds(p * wk, wk), :],
+                gu_sem.at[l, m, p],
             )
+            for l in range(own)
             for m, ref in enumerate((gw_ref, uw_ref))
         ]
 
@@ -100,21 +100,20 @@
             for l in range(own)
         ]
 
-    def gu_start(k, carry):
-        for l in range(own):
-            for copy in gu_copies(l, k):
+    def gu_start(low, high):
+        for p in range(low, min(high, pieces)):
+            for copy in gu_copies(p):
                 copy.start()
-        return carry
-
-    lax.fori_loop(0, nk, gu_start, 0)
 
     def dn_start(low, high):
         for c in range(low, min(high, nc)):
             for copy in dn_copies(c):
                 copy.start()
 
+    ahead = max(1, pieces - 1)
     for copy in load_own():
         copy.wait()
+    gu_start(0, ahead)
     lane = lax.broadcasted_iota(jnp.int32, (rows, LANES), 1)
     same = (
         lax.broadcasted_iota(jnp.int32, (rows, rows), 0)
@@ -134,69 +133,82 @@
 
     pl.semaphore_wait(barrier, greeted)
 
-    def send(p, slot, send_sem, device_id):
+    def send(p, slot, count, send_sem, recv_sem, device_id):
         span = pl.ds(0, wk + LANES if p == pieces - 1 else wk)
+        blocks = xg.at[p, pl.ds(slot, count), :, span]
         return pltpu.make_async_remote_copy(
-            src_ref=xg.at[p, slot, :, span], dst_ref=xg.at[p, slot, :, span],
-            send_sem=send_sem, recv_sem=g_recv.at[p, slot],
+            src_ref=blocks, dst_ref=blocks, send_sem=send_sem, recv_sem=recv_sem,
             device_id=device_id, device_id_type=MESH,
         )
 
-    def z_copy(p, d):
-        return send(p, me, zs.at[p, d], device(q, (z + d) % nz))
-
-    def q_copy(p, slot, i, d):
-        return send(p, slot, qs.at[p, d, i], device((q + d) % nq, z))
-
-    def e_copy(p, slot):
-        return send(p, slot, es.at[p, slot % nqz], {"exp": other})
-
-    def arrived(p, slot):
-        send(p, slot, zs.at[p, 0], {"exp": other}).wait_recv()
-
-    def pass_q(p, slot, i):
+    def z_copy(p, d, count=1):
+        return send(
+            p, me, count, g_send.at[0, p], z_recv.at[p, z], device(q, (z + d) % nz)
+        )
+
+    def q_copy(p, zz, d):
+        return send(
+            p, slot_of(e, q, zz), 1, g_send.at[1, p], g_recv.at[p, zz],
+            device((q + d) % nq, z),
+        )
+
+    def e_copy(p, zz):
+        return send(
+            p, slot_of(e, 0, zz), nq, g_send.at[2, p], e_recv.at[p], {"exp": other}
+        )
+
+    def await_z(p, zz):
+        send(p, 0, 1, g_send.at[0, p], z_recv.at[p, zz], {"exp": other}).wait_recv()
+
+    def await_q(p, zz):
+        send(p, 0, nq - 1, g_send.at[1, p], g_recv.at[p, zz], {"exp": other}).wait_recv()
+
+    def await_e(p):
+        send(p, 0, nqz, g_send.at[2, p], e_recv.at[p], {"exp": other}).wait_recv()
+
+    def gather_drain():
+        for p in range(pieces):
+            for i, count in enumerate((nz - 1, (nq - 1) * nz, nqz)):
+                send(p, 0, count, g_send.at[i, p], e_recv.at[p], {"exp": other}).wait_send()
+
+    def pass_q(p, zz):
         for d in range(1, nq):
-            q_copy(p, slot, i, d).start()
-        e_copy(p, slot).start()
-
-    for p in range(pieces):
+            q_copy(p, zz, d).start()
+
+    def z_start(p):
         for d in range(1, nz):
             z_copy(p, d).start()
-        pass_q(p, me, z)
 
     def z_relay(p):
         def go(i, carry):
             zz = near(i)
-            slot = slot_of(e, q, zz)
-            arrived(p, slot)
-            pass_q(p, slot, zz)
+            await_z(p, zz)
+            pass_q(p, zz)
             return carry
 
         lax.fori_loop(1, nz, go, 0)
 
-    def q_relay(p):
+    def q_relay(p, low, high):
         def go(i, carry):
-            zz = jnp.where(i // (nq - 1) == 0, z, near(i // (nq - 1)))
-            slot = slot_of(e, (q + 1 + i % (nq - 1)) % nq, zz)
-            arrived(p, slot)
-            e_copy(p, slot).start()
+            zz = jnp.where(i == 0, z, near(i))
+            await_q(p, zz)
+            e_copy(p, zz).start()
             return carry
 
-        lax.fori_loop(0, (nq - 1) * nz, go, 0)
-
-    def e_arrive(p):
-        def go(i, carry):
-            arrived(p, other * nqz + i)
-            return carry
-
-        lax.fori_loop(0, nqz, go, 0)
+        lax.fori_loop(low, high, go, 0)
+
+    z_start(0)
+    pass_q(0, z)
+    for p in range(1, pieces):
+        z_start(p)
 
     def lay(p, side):
         def go(g, carry):
-            slot = side * nqz + g * group
             for i in range(group):
-                stage[i * rows:(i + 1) * rows, :] = xg[p, slot + i].astype(jnp.float32)
-            r0 = pl.multiple_of(slot * rows, group * rows)
+                place = g * group + i
+                slot = slot_of(side, place // nz, place % nz)
+                stage[i * rows:(i + 1) * rows, :] = xg[p, slot].astype(jnp.float32)
+            r0 = pl.multiple_of(side * half + g * group * rows, group * rows)
             x[p, pl.ds(r0, group * rows), :] = stage[:, :wk].astype(jnp.bfloat16)
             if p == pieces - 1:
                 wst[pl.ds(r0, group * rows), :] = stage[:, wk:]
@@ -207,10 +219,9 @@
     step = 256
 
     def project(p):
+        for copy in gu_copies(p):
+            copy.wait()
         for l in range(own):
-            for k in range(p * nk // pieces, (p + 1) * nk // pieces):
-                for copy in gu_copies(l, k):
-                    copy.wait()
             for n in range(0, hidden, step):
                 cols = slice(n, min(n + step, hidden))
                 gate, upper = (
@@ -231,16 +242,18 @@
 
     for p in range(pieces):
         z_relay(p)
-    dn_start(0, 3)
+        if p == 0:
+            gu_start(ahead, pieces)
+            dn_start(0, 2)
+        if p + 1 < pieces:
+            pass_q(p + 1, z)
+    q_relay(0, 0, nz)
+    dn_start(2, nc)
     for p in range(pieces):
-        q_relay(p)
-        if p == 0:
-            dn_start(3, nc)
-            lay(p, e)
-    for p in range(pieces):
-        if p > 0:
-            lay(p, e)
-        e_arrive(p)
+        lay(p, e)
+        if p + 1 < pieces:
+            q_relay(p + 1, 0, nz)
+        await_e(p)
         lay(p, other)
         project(p)
 
@@ -254,7 +267,7 @@
     def ex_copy(c):
         return pltpu.make_async_remote_copy(
             src_ref=ex_send.at[c], dst_ref=ex_recv.at[c],
-            send_sem=ex_ssem.at[c], recv_sem=ex_rsem.at[c],
+            send_sem=s_send.at[0], recv_sem=ex_rsem.at[c],
             device_id={"exp": other}, device_id_type=MESH,
         )
 
@@ -262,7 +275,7 @@
         target = (q + d) % nq
         return pltpu.make_async_remote_copy(
             src_ref=q_send.at[c, target], dst_ref=q_recv.at[c, d],
-            send_sem=q_ssem.at[c, d], recv_sem=q_rsem.at[c, d],
+            send_sem=s_send.at[1], recv_sem=q_rsem.at[c],
             device_id=device(target, z), device_id_type=MESH,
         )
 
@@ -270,9 +283,25 @@
         target = (z + d) % nz
         return pltpu.make_async_remote_copy(
             src_ref=f_send.at[c, target], dst_ref=f_recv.at[c, d],
-            send_sem=f_ssem.at[c, d], recv_sem=f_rsem.at[c, d],
+            send_sem=s_send.at[2], recv_sem=f_rsem.at[c],
             device_id=device(q, target), device_id_type=MESH,
         )
+
+    def await_sum(buffer, recv_sem, c):
+        blocks = buffer.at[c, pl.ds(1, buffer.shape[1] - 1)]
+        pltpu.make_async_remote_copy(
+            src_ref=blocks, dst_ref=blocks, send_sem=s_send.at[0], recv_sem=recv_sem.at[c],
+            device_id={"exp": other}, device_id_type=MESH,
+        ).wait_recv()
+
+    def sum_drain():
+        for i, blocks in enumerate((
+            ex_send, q_send.at[:, pl.ds(1, nq - 1)], f_send.at[:, pl.ds(1, nz - 1)]
+        )):
+            pltpu.make_async_remote_copy(
+                src_ref=blocks, dst_ref=blocks, send_sem=s_send.at[i], recv_sem=ex_rsem.at[0],
+                device_id={"exp": other}, device_id_type=MESH,
+            ).wait_send()
 
     def down(c):
         for copy in dn_copies(c):
@@ -304,8 +333,8 @@
 
     def pass_q_sum(c):
         total = mine_q[c]
+        await_sum(q_recv, q_rsem, c)
         for d in range(1, nq):
-            sq_copy(c, d).wait_recv()
             total = total + q_recv[c, d].astype(jnp.float32)
         for j in range(nz):
             f_send[c, j] = total[j * rows:(j + 1) * rows, :].astype(jnp.bfloat16)
@@ -314,37 +343,11 @@
             f_copy(c, d).start()
 
     def collect(c):
-        for d in range(1, nz):
-            f_copy(c, d).wait_recv()
+        await_sum(f_recv, f_rsem, c)
         total = f_recv[c, 0].astype(jnp.float32)
         for d in range(1, nz):
             total += f_recv[c, d].astype(jnp.float32)
         out_ref[:, c * cw:(c + 1) * cw] = total.astype(out_ref.dtype)
-
-    def gather_drain():
-        for p in range(pieces):
-            for d in range(1, nz):
-                z_copy(p, d).wait_send()
-
-            def q_drain(i, carry, p=p):
-                for d in range(1, nq):
-                    q_copy(p, me, i, d).wait_send()
-                return carry
-
-            lax.fori_loop(0, nz, q_drain, 0)
-
-            def e_drain(i, carry, p=p):
-                e_copy(p, e * nqz + i).wait_send()
-                return carry
-
-            lax.fori_loop(0, nqz, e_drain, 0)
-
-    def sum_drain(c):
-        ex_copy(c).wait_send()
-        for d in range(1, nq):
-            sq_copy(c, d).wait_send()
-        for d in range(1, nz):
-            f_copy(c, d).wait_send()
 
     lag_ex, lag_q = 2, 6
     for c in range(nc + lag_q):
@@ -358,8 +361,7 @@
             pass_q_sum(c - lag_q)
     for c in range(nc):
         collect(c)
-    for c in range(nc):
-        sum_drain(c)
+    sum_drain()
 
 
 def body(tokens, expert_ids, gate_ints, gate_weight, up_weight, down_weight):
@@ -376,9 +378,8 @@
     slots = nt * nr * 2
     total = slots * rows
     pieces = 2
-    kc = min(512, width // pieces)
     cw = min(512, width)
-    nk, nc = width // kc, width // cw
+    nc = width // cw
     bf16, f32, i32 = jnp.bfloat16, jnp.float32, jnp.int32
     vmem = pl.BlockSpec(memory_space=pltpu.VMEM)
     hbm = pl.BlockSpec(memory_space=pl.ANY)
@@ -387,8 +388,8 @@
     part = total // 2 // nq
     top = expert_ids.shape[1]
     return pl.pallas_call(
-        functools.partial(kernel, (nr, ny, nz, own), kc, cw, pieces),
-        out_shape=jax.ShapeDtypeStruct((rows, width), bf16),
+        functools.partial(kernel, (nr, ny, nz, own), cw, pieces),
+        out_shape=pltpu.VMEM((rows, width), bf16),
         in_specs=[hbm] * 6,
         out_specs=vmem,
         scratch_shapes=[
@@ -411,18 +412,16 @@
             pltpu.VMEM((nc, nz, rows, cw), bf16),
             pltpu.VMEM((nc, nz, rows, cw), bf16),
             dma((2 + pieces,)),
-            dma((own, 2, nk)),
+            dma((own, 2, pieces)),
             dma((own, nc)),
+            dma((3, pieces)),
             dma((pieces, nz)),
-            dma((pieces, nq, nz)),
-            dma((pieces, nq * nz)),
-            dma((pieces, slots)),
+            dma((pieces, nz)),
+            dma((pieces,)),
+            dma((3,)),
             dma((nc,)),
             dma((nc,)),
-            dma((nc, nq)),
-            dma((nc, nq)),
-            dma((nc, nz)),
-            dma((nc, nz)),
+            dma((nc,)),
         ],
         compiler_params=pltpu.CompilerParams(
             collective_id=0, has_side_effects=True, vmem_limit_bytes=VMEM_BYTES

time: 37.3 us -> 34.4 us (0.922)
  Pallas kernels: 35.7 us -> 33.5 us
  local copies, waits for them, and re-layouts: 1.39 us -> 0.62 us
    pallas_call x1, Pallas kernels: 35.7 us -> 33.5 us  [body(): pl.pallas_call(functools.partial(kernel, (nr, ny, nz, own), cw, pieces),...]
    unnamed x1, local copies, waits for them, and re-layouts: 1.39 us -> 0.62 us
where the time goes in v4:
time: 34.4 us; the launch traced here: 34.2 us
  Pallas kernels  33.5 us (97%)
  local copies, waits for them, and re-layouts  0.62 us (2%)
    pallas_call x1, Pallas kernels, body(): pl.pallas_call(functools.partial(kernel, (nr, ny, nz, own), cw, pieces),...  33.5 us

profile of v4, /device:TPU:0, one launch (start us, length us, event | category | flops | bytes accessed | tf_op | source)
XLA Modules:
  0.0 34.2 jit_solution(17032645068935385482)
XLA Ops:
  0.0 33.5 %shard_map.64 = bf16[4,4096]{1,0:T(4,128)(2,1)S(1)} custom-call(s32[2,4]{1,0:T(2,128)} %bitcast.2, s32[2,4]{1,0:T(2,128)} %bitcast.3, bf16[4,4096]{1,0:T(4,128)(2,1)} %tok_hbm.1, bf16[2,4096,1792]{2,1,0:T(8,128)(2,1)} %gw_ref.1, bf16[2,4096,1792]{2,1,0:T(8,128)(2,1)} %uw_ref.1, bf16[2,1792,4096]{2,1,0:T(8,128)(2,1)} %dw_ref.1), custom_call_target="tpu_custom_call" | custom-call | tf_op jit(solution)/shard_map/pallas_call | solution.py:390
  33.6 0.6 %copy.8 = bf16[4,4096]{1,0:T(4,128)(2,1)} copy(bf16[4,4096]{1,0:T(4,128)(2,1)S(1)} %shard_map.64) | data formatting | bytes 65536

commit v5 on v4

--- a/solution.py
+++ b/solution.py
@@ -13,9 +13,9 @@
 
 
 def kernel(
-    dims, cw, pieces,
+    dims, cw, pieces, early,
     ids_hbm, gates_hbm, tok_hbm, gw_ref, uw_ref, dw_ref, out_ref,
-    ids_ref, gates_ref, xg, stage, x, wst, acc, h, wbuf, dbuf, keep, mine_q,
+    ids_ref, gates_ref, xg, stage, x, wst, acc, h, wbuf, dbuf, keep,
     ex_send, ex_recv, q_send, q_recv, f_send, f_recv,
     in_sem, gu_sem, dn_sem, g_send, z_recv, g_recv, e_recv,
     s_send, ex_rsem, q_rsem, f_rsem,
@@ -30,11 +30,12 @@
     rows, width = tok_hbm.shape
     hidden = gw_ref.shape[2]
     experts = gw_ref.shape[0]
-    tokens = x.shape[1]
+    tokens = x.shape[0]
     half = tokens // 2
     part = half // nq
     nc = width // cw
-    wk = width // pieces
+    spans = [slice(low * width // pieces[-1], high * width // pieces[-1]) for low, high in zip(pieces, pieces[1:])]
+    pieces = len(spans)
     group = stage.shape[0] // rows
     nqz = nq * nz
 
@@ -43,6 +44,11 @@
 
     def device(qq, zz):
         return {"rep": qq // ny, "tp": zz * ny + qq % ny}
+
+    a, b = q // ny + e * (q % ny - q // ny), q % ny + e * (q // ny - q % ny)
+
+    def crossed(aa, bb):
+        return aa * (ny + e * (1 - ny)) + bb * (1 + e * (ny - 1))
 
     def near(i):
         m = jnp.minimum(z, nz - 1 - z)
@@ -70,9 +76,9 @@
     def load_own():
         copies = [
             pltpu.make_async_copy(
-                tok_hbm.at[:, pl.ds(p * wk, wk)], xg.at[p, me, :, pl.ds(0, wk)], in_sem.at[2 + p]
+                tok_hbm.at[:, span], xg.at[me, :, span], in_sem.at[2 + p]
             )
-            for p in range(pieces)
+            for p, span in enumerate(spans)
         ]
         copies.append(pltpu.make_async_copy(ids_hbm, ids_ref, in_sem.at[0]))
         copies.append(pltpu.make_async_copy(gates_hbm, gates_ref, in_sem.at[1]))
@@ -84,8 +90,8 @@
     def gu_copies(p):
         return [
             pltpu.make_async_copy(
-                ref.at[r * own + l, pl.ds(p * wk, wk), :],
-                wbuf.at[l, m, pl.ds(p * wk, wk), :],
+                ref.at[r * own + l, spans[p], :],
+                wbuf.at[l, m, spans[p], :],
                 gu_sem.at[l, m, p],
             )
             for l in range(own)
@@ -129,13 +135,13 @@
             for ref in (ids_ref, gates_ref)
         )
         weight += jnp.where(lane.astype(jnp.float32) == ids, gates * (1.0 / 256.0), 0.0)
-    xg[pieces - 1, me, :, wk:] = weight.astype(jnp.bfloat16)
+    xg[me, :, width:] = weight.astype(jnp.bfloat16)
 
     pl.semaphore_wait(barrier, greeted)
 
     def send(p, slot, count, send_sem, recv_sem, device_id):
-        span = pl.ds(0, wk + LANES if p == pieces - 1 else wk)
-        blocks = xg.at[p, pl.ds(slot, count), :, span]
+        span = slice(spans[p].start, width + LANES) if p == pieces - 1 else spans[p]
+        blocks = xg.at[pl.ds(slot, count), :, span]
         return pltpu.make_async_remote_copy(
             src_ref=blocks, dst_ref=blocks, send_sem=send_sem, recv_sem=recv_sem,
             device_id=device_id, device_id_type=MESH,
@@ -203,15 +209,17 @@
         z_start(p)
 
     def lay(p, side):
+        low, high = spans[p].start, spans[p].stop + (LANES if p == pieces - 1 else 0)
+
         def go(g, carry):
             for i in range(group):
                 place = g * group + i
                 slot = slot_of(side, place // nz, place % nz)
-                stage[i * rows:(i + 1) * rows, :] = xg[p, slot].astype(jnp.float32)
+                stage[i * rows:(i + 1) * rows, low:high] = xg[slot, :, low:high].astype(jnp.float32)
             r0 = pl.multiple_of(side * half + g * group * rows, group * rows)
-            x[p, pl.ds(r0, group * rows), :] = stage[:, :wk].astype(jnp.bfloat16)
+            x[pl.ds(r0, group * rows), spans[p]] = stage[:, spans[p]].astype(jnp.bfloat16)
             if p == pieces - 1:
-                wst[pl.ds(r0, group * rows), :] = stage[:, wk:]
+                wst[pl.ds(r0, group * rows), :] = stage[:, width:]
             return carry
 
         lax.fori_loop(0, half // (group * rows), go, 0)
@@ -226,7 +234,7 @@
                 cols = slice(n, min(n + step, hidden))
                 gate, upper = (
                     jnp.dot(
-                        x[p], wbuf[l, m, p * wk:(p + 1) * wk, cols],
+                        x[:, spans[p]], wbuf[l, m, spans[p], cols],
                         preferred_element_type=jnp.float32,
                     )
                     for m in range(2)
@@ -271,97 +279,135 @@
             device_id={"exp": other}, device_id_type=MESH,
         )
 
-    def sq_copy(c, d):
-        target = (q + d) % nq
+    def sq_copies(c):
+        if c < early:
+            pairs = [
+                (crossed((a + d) % nr, i), d * nr + i, crossed((a + d) % nr, b))
+                for d in range(1, nr)
+                for i in range(nr)
+            ]
+        else:
+            pairs = [((q + d) % nq, d, (q + d) % nq) for d in range(1, nq)]
+        return [
+            pltpu.make_async_remote_copy(
+                src_ref=q_send.at[c, block], dst_ref=q_recv.at[c, place],
+                send_sem=s_send.at[1], recv_sem=q_rsem.at[c],
+                device_id=device(target, z), device_id_type=MESH,
+            )
+            for block, place, target in pairs
+        ]
+
+    def f_copy(c, d):
+        if c < early:
+            place = (b * nz + z + d) % (nr * nz)
+            target = device(crossed(a, place // nz), place % nz)
+        else:
+            place = (z + d) % nz
+            target = device(q, place)
         return pltpu.make_async_remote_copy(
-            src_ref=q_send.at[c, target], dst_ref=q_recv.at[c, d],
-            send_sem=s_send.at[1], recv_sem=q_rsem.at[c],
-            device_id=device(target, z), device_id_type=MESH,
-        )
-
-    def f_copy(c, d):
-        target = (z + d) % nz
+            src_ref=f_send.at[c, place], dst_ref=f_recv.at[c, d],
+            send_sem=s_send.at[2], recv_sem=f_rsem.at[c],
+            device_id=target, device_id_type=MESH,
+        )
+
+    def q_count(c):
+        return (nr - 1) * nr if c < early else nq - 1
+
+    def f_count(c):
+        return nr * nz if c < early else nz
+
+    def some(buffer, c, count, i, recv_sem):
+        blocks = buffer.at[c, pl.ds(0, count)]
         return pltpu.make_async_remote_copy(
-            src_ref=f_send.at[c, target], dst_ref=f_recv.at[c, d],
-            send_sem=s_send.at[2], recv_sem=f_rsem.at[c],
-            device_id=device(q, target), device_id_type=MESH,
-        )
-
-    def await_sum(buffer, recv_sem, c):
-        blocks = buffer.at[c, pl.ds(1, buffer.shape[1] - 1)]
-        pltpu.make_async_remote_copy(
-            src_ref=blocks, dst_ref=blocks, send_sem=s_send.at[0], recv_sem=recv_sem.at[c],
+            src_ref=blocks, dst_ref=blocks, send_sem=s_send.at[i], recv_sem=recv_sem.at[c],
             device_id={"exp": other}, device_id_type=MESH,
-        ).wait_recv()
-
-    def sum_drain():
-        for i, blocks in enumerate((
-            ex_send, q_send.at[:, pl.ds(1, nq - 1)], f_send.at[:, pl.ds(1, nz - 1)]
-        )):
-            pltpu.make_async_remote_copy(
-                src_ref=blocks, dst_ref=blocks, send_sem=s_send.at[i], recv_sem=ex_rsem.at[0],
-                device_id={"exp": other}, device_id_type=MESH,
-            ).wait_send()
-
-    def down(c):
-        for copy in dn_copies(c):
-            copy.wait()
-        for n in range(0, cw, step):
-            cols = slice(n, min(n + step, cw))
-            total = None
-            for l in range(own):
-                value = scales[l] * jnp.dot(
-                    h[l], dbuf[l, c, :, cols], preferred_element_type=jnp.float32
-                )
-                total = value if total is None else total + value
-            low, high = total[:half], total[half:]
-            keep[c, :, cols] = jnp.where(e == 0, low, high)
-            ex_send[c, :, cols] = jnp.where(e == 0, high, low).astype(jnp.bfloat16)
-        ex_copy(c).start()
+        )
+
+    def sum_drain(low, high):
+        for c in range(low, high):
+            ex_copy(c).wait_send()
+            some(q_send, c, q_count(c), 1, q_rsem).wait_send()
+            some(f_send, c, f_count(c) - 1, 2, f_rsem).wait_send()
+
+    def down(chunks):
+        for c in chunks:
+            for copy in dn_copies(c):
+                copy.wait()
+        for c in chunks:
+            for n in range(0, cw, step):
+                cols = slice(n, min(n + step, cw))
+                total = None
+                for l in range(own):
+                    value = scales[l] * jnp.dot(
+                        h[l], dbuf[l, c, :, cols], preferred_element_type=jnp.float32
+                    )
+                    total = value if total is None else total + value
+                low, high = total[:half], total[half:]
+                keep[c, :, cols] = jnp.where(e == 0, low, high)
+                ex_send[c, :, cols] = jnp.where(e == 0, high, low).astype(jnp.bfloat16)
+        for c in chunks:
+            ex_copy(c).start()
 
     def pass_ex(c):
         ex_copy(c).wait_recv()
-        picked = None
         for qq in range(nq):
             span = slice(qq * part, (qq + 1) * part)
             total = keep[c, span, :] + ex_recv[c, span, :].astype(jnp.float32)
             q_send[c, qq] = total.astype(jnp.bfloat16)
-            picked = total if picked is None else jnp.where(q == qq, total, picked)
-        mine_q[c] = picked
-        for d in range(1, nq):
-            sq_copy(c, d).start()
+            keep[c, span, :] = total
+        for copy in sq_copies(c):
+            copy.start()
+
+    def kept(c, block):
+        return keep[c, pl.ds(pl.multiple_of(block * part, part), part), :]
 
     def pass_q_sum(c):
-        total = mine_q[c]
-        await_sum(q_recv, q_rsem, c)
-        for d in range(1, nq):
-            total = total + q_recv[c, d].astype(jnp.float32)
-        for j in range(nz):
-            f_send[c, j] = total[j * rows:(j + 1) * rows, :].astype(jnp.bfloat16)
-        f_recv[c, 0] = f_send[c, z]
-        for d in range(1, nz):
+        some(q_recv, c, q_count(c), 1, q_rsem).wait_recv()
+        if c < early:
+            sums = [
+                sum(
+                    (q_recv[c, d * nr + i].astype(jnp.float32) for d in range(1, nr)),
+                    start=kept(c, crossed(a, i)),
+                )
+                for i in range(nr)
+            ]
+            mine = b * nz + z
+        else:
+            sums = [
+                sum((q_recv[c, d].astype(jnp.float32) for d in range(1, nq)), start=kept(c, q))
+            ]
+            mine = z
+        for i, total in enumerate(sums):
+            for j in range(nz):
+                f_send[c, i * nz + j] = total[j * rows:(j + 1) * rows, :].astype(jnp.bfloat16)
+        f_recv[c, 0] = f_send[c, mine]
+        for d in range(1, f_count(c)):
             f_copy(c, d).start()
 
     def collect(c):
-        await_sum(f_recv, f_rsem, c)
+        some(f_recv, c, f_count(c) - 1, 2, f_rsem).wait_recv()
         total = f_recv[c, 0].astype(jnp.float32)
-        for d in range(1, nz):
+        for d in range(1, f_count(c)):
             total += f_recv[c, d].astype(jnp.float32)
         out_ref[:, c * cw:(c + 1) * cw] = total.astype(out_ref.dtype)
 
-    lag_ex, lag_q = 2, 6
-    for c in range(nc + lag_q):
-        if c < nc:
-            down(c)
-        if lag_ex <= c < nc + lag_ex:
-            pass_ex(c - lag_ex)
-        if c == nc:
-            gather_drain()
-        if c >= lag_q:
-            pass_q_sum(c - lag_q)
+    groups = [range(c, min(c + 2, nc)) for c in range(0, nc, 2)]
+    for i, chunks in enumerate(groups):
+        down(chunks)
+        if i >= 2:
+            for c in groups[i - 2]:
+                pass_ex(c)
+    gather_drain()
+    for chunks in groups[-2:]:
+        for c in chunks:
+            pass_ex(c)
     for c in range(nc):
+        pass_q_sum(c)
+    for c in range(nc):
+        if c == nc - 1:
+            sum_drain(0, nc - 1)
         collect(c)
-    sum_drain()
+    sum_drain(nc - 1, nc)
 
 
 def body(tokens, expert_ids, gate_ints, gate_weight, up_weight, down_weight):
@@ -377,9 +423,12 @@
     own = experts // nr
     slots = nt * nr * 2
     total = slots * rows
-    pieces = 2
+    cuts = (0, 1, 2, 4)
+    pieces = len(cuts) - 1
     cw = min(512, width)
     nc = width // cw
+    early = nc // 2 if nr == ny else 0
+    ends = nt if early else nz
     bf16, f32, i32 = jnp.bfloat16, jnp.float32, jnp.int32
     vmem = pl.BlockSpec(memory_space=pltpu.VMEM)
     hbm = pl.BlockSpec(memory_space=pl.ANY)
@@ -388,29 +437,28 @@
     part = total // 2 // nq
     top = expert_ids.shape[1]
     return pl.pallas_call(
-        functools.partial(kernel, (nr, ny, nz, own), cw, pieces),
+        functools.partial(kernel, (nr, ny, nz, own), cw, cuts, early),
         out_shape=pltpu.VMEM((rows, width), bf16),
         in_specs=[hbm] * 6,
         out_specs=vmem,
         scratch_shapes=[
             pltpu.VMEM((top, rows), i32),
             pltpu.VMEM((top, rows), i32),
-            pltpu.VMEM((pieces, slots, rows, width // pieces + LANES), bf16),
-            pltpu.VMEM((16, width // pieces + LANES), f32),
-            pltpu.VMEM((pieces, total, width // pieces), bf16),
+            pltpu.VMEM((slots, rows, width + LANES), bf16),
+            pltpu.VMEM((16, width + LANES), f32),
+            pltpu.VMEM((total, width), bf16),
             pltpu.VMEM((total, LANES), f32),
             pltpu.VMEM((own, 2, total, hidden), f32),
             pltpu.VMEM((own, total, hidden), bf16),
             pltpu.VMEM((own, 2, width, hidden), bf16),
             pltpu.VMEM((own, nc, hidden, cw), bf16),
             pltpu.VMEM((nc, total // 2, cw), f32),
-            pltpu.VMEM((nc, part, cw), f32),
             pltpu.VMEM((nc, total // 2, cw), bf16),
             pltpu.VMEM((nc, total // 2, cw), bf16),
             pltpu.VMEM((nc, nq, part, cw), bf16),
             pltpu.VMEM((nc, nq, part, cw), bf16),
-            pltpu.VMEM((nc, nz, rows, cw), bf16),
-            pltpu.VMEM((nc, nz, rows, cw), bf16),
+            pltpu.VMEM((nc, ends, rows, cw), bf16),
+            pltpu.VMEM((nc, ends, rows, cw), bf16),
             dma((2 + pieces,)),
             dma((own, 2, pieces)),
             dma((own, nc)),

time: 34.4 us -> 33.4 us (0.971)
  Pallas kernels: 33.5 us -> 32.6 us
    pallas_call x1, Pallas kernels: 33.5 us -> 32.6 us  [body(): pl.pallas_call(functools.partial(kernel, (nr, ny, nz, own), cw, cuts, ear...]
where the time goes in v5:
time: 33.4 us; the launch traced here: 33.2 us
  Pallas kernels  32.6 us (98%)
  local copies, waits for them, and re-layouts  0.62 us (2%)
    pallas_call x1, Pallas kernels, body(): pl.pallas_call(functools.partial(kernel, (nr, ny, nz, own), cw, cuts, ear...  32.6 us

profile of v5, /device:TPU:0, one launch (start us, length us, event | category | flops | bytes accessed | tf_op | source)
XLA Modules:
  0.0 33.2 jit_solution(822832613992396347)
XLA Ops:
  0.0 32.6 %shard_map.64 = bf16[4,4096]{1,0:T(4,128)(2,1)S(1)} custom-call(s32[2,4]{1,0:T(2,128)} %bitcast.2, s32[2,4]{1,0:T(2,128)} %bitcast.3, bf16[4,4096]{1,0:T(4,128)(2,1)} %tok_hbm.1, bf16[2,4096,1792]{2,1,0:T(8,128)(2,1)} %gw_ref.1, bf16[2,4096,1792]{2,1,0:T(8,128)(2,1)} %uw_ref.1, bf16[2,1792,4096]{2,1,0:T(8,128)(2,1)} %dw_ref.1), custom_call_target="tpu_custom_call" | custom-call | tf_op jit(solution)/shard_map/pallas_call | solution.py:439
  32.6 0.6 %copy.8 = bf16[4,4096]{1,0:T(4,128)(2,1)} copy(bf16[4,4096]{1,0:T(4,128)(2,1)S(1)} %shard_map.64) | data formatting | bytes 65536

commit v6 on v5

--- a/solution.py
+++ b/solution.py
@@ -92,7 +92,7 @@
             pltpu.make_async_copy(
                 ref.at[r * own + l, spans[p], :],
                 wbuf.at[l, m, spans[p], :],
-                gu_sem.at[l, m, p],
+                gu_sem.at[l, p],
             )
             for l in range(own)
             for m, ref in enumerate((gw_ref, uw_ref))
@@ -101,7 +101,7 @@
     def dn_copies(c):
         return [
             pltpu.make_async_copy(
-                dw_ref.at[r * own + l, :, pl.ds(c * cw, cw)], dbuf.at[l, c], dn_sem.at[l, c]
+                dw_ref.at[r * own + l, :, pl.ds(c * cw, cw)], dbuf.at[l, c], dn_sem.at[l, c // 2]
             )
             for l in range(own)
         ]
@@ -120,6 +120,77 @@
     for copy in load_own():
         copy.wait()
     gu_start(0, ahead)
+    pl.semaphore_wait(barrier, greeted)
+
+    def send(p, slot, count, send_sem, recv_sem, device_id):
+        span = slice(spans[p].start, width + LANES) if p == pieces - 1 else spans[p]
+        blocks = xg.at[pl.ds(slot, count), :, span]
+        return pltpu.make_async_remote_copy(
+            src_ref=blocks, dst_ref=blocks, send_sem=send_sem, recv_sem=recv_sem,
+            device_id=device_id, device_id_type=MESH,
+        )
+
+    def z_copy(p, d, count=1):
+        return send(
+            p, me, count, g_send.at[0], z_recv.at[p, z], device(q, (z + d) % nz)
+        )
+
+    def q_copy(p, zz, d):
+        return send(
+            p, slot_of(e, q, zz), 1, g_send.at[1], g_recv.at[p, zz],
+            device((q + d) % nq, z),
+        )
+
+    def e_copy(p, zz):
+        return send(
+            p, slot_of(e, 0, zz), nq, g_send.at[2], e_recv.at[p], {"exp": other}
+        )
+
+    def await_z(p, zz):
+        send(p, 0, 1, g_send.at[0], z_recv.at[p, zz], {"exp": other}).wait_recv()
+
+    def await_q(p, zz):
+        send(p, 0, nq - 1, g_send.at[1], g_recv.at[p, zz], {"exp": other}).wait_recv()
+
+    def await_e(p):
+        send(p, 0, nqz, g_send.at[2], e_recv.at[p], {"exp": other}).wait_recv()
+
+    def gather_drain():
+        for i, count in enumerate((nz - 1, (nq - 1) * nz, nqz)):
+            whole = xg.at[pl.ds(0, count)]
+            pltpu.make_async_remote_copy(
+                src_ref=whole, dst_ref=whole, send_sem=g_send.at[i], recv_sem=e_recv.at[0],
+                device_id={"exp": other}, device_id_type=MESH,
+            ).wait_send()
+
+    def pass_q(p, zz):
+        for d in range(1, nq):
+            q_copy(p, zz, d).start()
+
+    def z_start(p):
+        for d in range(1, nz):
+            z_copy(p, d).start()
+
+    def z_relay(p):
+        def go(i, carry):
+            zz = near(i)
+            await_z(p, zz)
+            pass_q(p, zz)
+            return carry
+
+        lax.fori_loop(1, nz, go, 0)
+
+    def q_relay(p, low, high):
+        def go(i, carry):
+            zz = jnp.where(i == 0, z, near(i))
+            await_q(p, zz)
+            e_copy(p, zz).start()
+            return carry
+
+        lax.fori_loop(low, high, go, 0)
+
+    z_start(0)
+    pass_q(0, z)
     lane = lax.broadcasted_iota(jnp.int32, (rows, LANES), 1)
     same = (
         lax.broadcasted_iota(jnp.int32, (rows, rows), 0)
@@ -136,75 +207,6 @@
         )
         weight += jnp.where(lane.astype(jnp.float32) == ids, gates * (1.0 / 256.0), 0.0)
     xg[me, :, width:] = weight.astype(jnp.bfloat16)
-
-    pl.semaphore_wait(barrier, greeted)
-
-    def send(p, slot, count, send_sem, recv_sem, device_id):
-        span = slice(spans[p].start, width + LANES) if p == pieces - 1 else spans[p]
-        blocks = xg.at[pl.ds(slot, count), :, span]
-        return pltpu.make_async_remote_copy(
-            src_ref=blocks, dst_ref=blocks, send_sem=send_sem, recv_sem=recv_sem,
-            device_id=device_id, device_id_type=MESH,
-        )
-
-    def z_copy(p, d, count=1):
-        return send(
-            p, me, count, g_send.at[0, p], z_recv.at[p, z], device(q, (z + d) % nz)
-        )
-
-    def q_copy(p, zz, d):
-        return send(
-            p, slot_of(e, q, zz), 1, g_send.at[1, p], g_recv.at[p, zz],
-            device((q + d) % nq, z),
-        )
-
-    def e_copy(p, zz):
-        return send(
-            p, slot_of(e, 0, zz), nq, g_send.at[2, p], e_recv.at[p], {"exp": other}
-        )
-
-    def await_z(p, zz):
-        send(p, 0, 1, g_send.at[0, p], z_recv.at[p, zz], {"exp": other}).wait_recv()
-
-    def await_q(p, zz):
-        send(p, 0, nq - 1, g_send.at[1, p], g_recv.at[p, zz], {"exp": other}).wait_recv()
-
-    def await_e(p):
-        send(p, 0, nqz, g_send.at[2, p], e_recv.at[p], {"exp": other}).wait_recv()
-
-    def gather_drain():
-        for p in range(pieces):
-            for i, count in enumerate((nz - 1, (nq - 1) * nz, nqz)):
-                send(p, 0, count, g_send.at[i, p], e_recv.at[p], {"exp": other}).wait_send()
-
-    def pass_q(p, zz):
-        for d in range(1, nq):
-            q_copy(p, zz, d).start()
-
-    def z_start(p):
-        for d in range(1, nz):
-            z_copy(p, d).start()
-
-    def z_relay(p):
-        def go(i, carry):
-            zz = near(i)
-            await_z(p, zz)
-            pass_q(p, zz)
-            return carry
-
-        lax.fori_loop(1, nz, go, 0)
-
-    def q_relay(p, low, high):
-        def go(i, carry):
-            zz = jnp.where(i == 0, z, near(i))
-            await_q(p, zz)
-            e_copy(p, zz).start()
-            return carry
-
-        lax.fori_loop(low, high, go, 0)
-
-    z_start(0)
-    pass_q(0, z)
     for p in range(1, pieces):
         z_start(p)
 
@@ -222,13 +224,19 @@
                 wst[pl.ds(r0, group * rows), :] = stage[:, width:]
             return carry
 
-        lax.fori_loop(0, half // (group * rows), go, 0)
+        steps = half // (group * rows)
+        if steps > 8:
+            lax.fori_loop(0, steps, go, 0)
+        else:
+            for g in range(steps):
+                go(g, 0)
 
     step = 256
 
     def project(p):
-        for copy in gu_copies(p):
-            copy.wait()
+        for l in range(own):
+            both = wbuf.at[l, :, spans[p], :]
+            pltpu.make_async_copy(both, both, gu_sem.at[l, p]).wait()
         for l in range(own):
             for n in range(0, hidden, step):
                 cols = slice(n, min(n + step, hidden))
@@ -257,12 +265,14 @@
             pass_q(p + 1, z)
     q_relay(0, 0, nz)
     dn_start(2, nc)
+    lay(0, e)
     for p in range(pieces):
-        lay(p, e)
         if p + 1 < pieces:
             q_relay(p + 1, 0, nz)
         await_e(p)
         lay(p, other)
+        if p + 1 < pieces:
+            lay(p + 1, e)
         project(p)
 
     lanes = lax.broadcasted_iota(jnp.int32, (tokens, LANES), 1)
@@ -275,7 +285,7 @@
     def ex_copy(c):
         return pltpu.make_async_remote_copy(
             src_ref=ex_send.at[c], dst_ref=ex_recv.at[c],
-            send_sem=s_send.at[0], recv_sem=ex_rsem.at[c],
+            send_sem=s_send.at[0], recv_sem=ex_rsem.at[c // 2],
             device_id={"exp": other}, device_id_type=MESH,
         )
 
@@ -330,9 +340,9 @@
             some(f_send, c, f_count(c) - 1, 2, f_rsem).wait_send()
 
     def down(chunks):
-        for c in chunks:
-            for copy in dn_copies(c):
-                copy.wait()
+        for l in range(own):
+            both = dbuf.at[l, pl.ds(chunks[0], len(chunks))]
+            pltpu.make_async_copy(both, both, dn_sem.at[l, chunks[0] // 2]).wait()
         for c in chunks:
             for n in range(0, cw, step):
                 cols = slice(n, min(n + step, cw))
@@ -348,8 +358,14 @@
         for c in chunks:
             ex_copy(c).start()
 
+    def await_ex(chunks):
+        blocks = ex_recv.at[pl.ds(chunks[0], len(chunks))]
+        pltpu.make_async_remote_copy(
+            src_ref=blocks, dst_ref=blocks, send_sem=s_send.at[0],
+            recv_sem=ex_rsem.at[chunks[0] // 2], device_id={"exp": other}, device_id_type=MESH,
+        ).wait_recv()
+
     def pass_ex(c):
-        ex_copy(c).wait_recv()
         for qq in range(nq):
             span = slice(qq * part, (qq + 1) * part)
             total = keep[c, span, :] + ex_recv[c, span, :].astype(jnp.float32)
@@ -395,10 +411,12 @@
     for i, chunks in enumerate(groups):
         down(chunks)
         if i >= 2:
+            await_ex(groups[i - 2])
             for c in groups[i - 2]:
                 pass_ex(c)
     gather_drain()
     for chunks in groups[-2:]:
+        await_ex(chunks)
         for c in chunks:
             pass_ex(c)
     for c in range(nc):
@@ -460,14 +478,14 @@
             pltpu.VMEM((nc, ends, rows, cw), bf16),
             pltpu.VMEM((nc, ends, rows, cw), bf16),
             dma((2 + pieces,)),
-            dma((own, 2, pieces)),
-            dma((own, nc)),
-            dma((3, pieces)),
+            dma((own, pieces)),
+            dma((own, -(-nc // 2))),
+            dma((3,)),
             dma((pieces, nz)),
             dma((pieces, nz)),
             dma((pieces,)),
             dma((3,)),
-            dma((nc,)),
+            dma((-(-nc // 2),)),
             dma((nc,)),
             dma((nc,)),
         ],

time: 33.4 us -> 33 us (0.988)
  Pallas kernels: 32.6 us -> 32.2 us
    pallas_call x1, Pallas kernels: 32.6 us -> 32.2 us  [body(): pl.pallas_call(functools.partial(kernel, (nr, ny, nz, own), cw, cuts, ear...]
where the time goes in v6:
time: 33 us; the launch traced here: 32.8 us
  Pallas kernels  32.2 us (98%)
  local copies, waits for them, and re-layouts  0.62 us (2%)
    pallas_call x1, Pallas kernels, body(): pl.pallas_call(functools.partial(kernel, (nr, ny, nz, own), cw, cuts, ear...  32.2 us

profile of v6, /device:TPU:0, one launch (start us, length us, event | category | flops | bytes accessed | tf_op | source)
XLA Modules:
  0.0 32.8 jit_solution(668484617077228486)
XLA Ops:
  0.0 32.2 %shard_map.64 = bf16[4,4096]{1,0:T(4,128)(2,1)S(1)} custom-call(s32[2,4]{1,0:T(2,128)} %bitcast.2, s32[2,4]{1,0:T(2,128)} %bitcast.3, bf16[4,4096]{1,0:T(4,128)(2,1)} %tok_hbm.1, bf16[2,4096,1792]{2,1,0:T(8,128)(2,1)} %gw_ref.1, bf16[2,4096,1792]{2,1,0:T(8,128)(2,1)} %uw_ref.1, bf16[2,1792,4096]{2,1,0:T(8,128)(2,1)} %dw_ref.1), custom_call_target="tpu_custom_call" | custom-call | tf_op jit(solution)/shard_map/pallas_call | solution.py:457
  32.2 0.6 %copy.8 = bf16[4,4096]{1,0:T(4,128)(2,1)} copy(bf16[4,4096]{1,0:T(4,128)(2,1)S(1)} %shard_map.64) | data formatting | bytes 65536

commit v7 on v6

--- a/solution.py
+++ b/solution.py
@@ -56,6 +56,15 @@
         one = jnp.where(z < nz - 1 - z, 1, -1) * (i - m)
         return z + jnp.where(i <= 2 * m, both, one)
 
+    moves = sorted(
+        ((dr, dy) for dr in range(nr) for dy in range(ny) if dr or dy),
+        key=lambda move: -sum(i > 0 for i in move),
+    )
+
+    def moved(d):
+        dr, dy = moves[d - 1]
+        return (q // ny + dr) % nr * ny + (q % ny + dy) % ny
+
     me = slot_of(e, q, z)
 
     barrier = pltpu.get_barrier_semaphore()
@@ -132,13 +141,13 @@
 
     def z_copy(p, d, count=1):
         return send(
-            p, me, count, g_send.at[0], z_recv.at[p, z], device(q, (z + d) % nz)
+            p, me, count, g_send.at[0], z_recv.at[p, z], device(q, near(nz - d))
         )
 
     def q_copy(p, zz, d):
         return send(
             p, slot_of(e, q, zz), 1, g_send.at[1], g_recv.at[p, zz],
-            device((q + d) % nq, z),
+            device(moved(d), z),
         )
 
     def e_copy(p, zz):
@@ -297,7 +306,7 @@
                 for i in range(nr)
             ]
         else:
-            pairs = [((q + d) % nq, d, (q + d) % nq) for d in range(1, nq)]
+            pairs = [(moved(d), d, moved(d)) for d in range(1, nq)]
         return [
             pltpu.make_async_remote_copy(
                 src_ref=q_send.at[c, block], dst_ref=q_recv.at[c, place],
@@ -312,8 +321,9 @@
             place = (b * nz + z + d) % (nr * nz)
             target = device(crossed(a, place // nz), place % nz)
         else:
-            place = (z + d) % nz
+            place = near(nz - d)
             target = device(q, place)
+            d = (place - z + nz) % nz
         return pltpu.make_async_remote_copy(
             src_ref=f_send.at[c, place], dst_ref=f_recv.at[c, d],
             send_sem=s_send.at[2], recv_sem=f_rsem.at[c],
@@ -443,9 +453,9 @@
     total = slots * rows
     cuts = (0, 1, 2, 4)
     pieces = len(cuts) - 1
-    cw = min(512, width)
+    cw = min(256, width)
     nc = width // cw
-    early = nc // 2 if nr == ny else 0
+    early = nc * 5 // 8 if nr == ny else 0
     ends = nt if early else nz
     bf16, f32, i32 = jnp.bfloat16, jnp.float32, jnp.int32
     vmem = pl.BlockSpec(memory_space=pltpu.VMEM)

time: 33 us -> 32.7 us (level)
  Pallas kernels: 32.2 us -> 31.8 us
    pallas_call x1, Pallas kernels: 32.2 us -> 31.8 us  [body(): pl.pallas_call(functools.partial(kernel, (nr, ny, nz, own), cw, cuts, ear...]
where the time goes in v7:
time: 32.7 us; the launch traced here: 32.5 us
  Pallas kernels  31.8 us (97%)
  local copies, waits for them, and re-layouts  0.62 us (2%)
    pallas_call x1, Pallas kernels, body(): pl.pallas_call(functools.partial(kernel, (nr, ny, nz, own), cw, cuts, ear...  31.8 us

profile of v7, /device:TPU:0, one launch (start us, length us, event | category | flops | bytes accessed | tf_op | source)
XLA Modules:
  0.0 32.5 jit_solution(5990140633071726980)
XLA Ops:
  0.0 31.8 %shard_map.64 = bf16[4,4096]{1,0:T(4,128)(2,1)S(1)} custom-call(s32[2,4]{1,0:T(2,128)} %bitcast.2, s32[2,4]{1,0:T(2,128)} %bitcast.3, bf16[4,4096]{1,0:T(4,128)(2,1)} %tok_hbm.1, bf16[2,4096,1792]{2,1,0:T(8,128)(2,1)} %gw_ref.1, bf16[2,4096,1792]{2,1,0:T(8,128)(2,1)} %uw_ref.1, bf16[2,1792,4096]{2,1,0:T(8,128)(2,1)} %dw_ref.1), custom_call_target="tpu_custom_call" | custom-call | tf_op jit(solution)/shard_map/pallas_call | solution.py:467
  31.8 0.6 %copy.8 = bf16[4,4096]{1,0:T(4,128)(2,1)} copy(bf16[4,4096]{1,0:T(4,128)(2,1)S(1)} %shard_map.64) | data formatting | bytes 65536
